TPU v7x, 32 devices: a whole 2x2x4 slice. The times are simulated.
32 devices in a mesh: req: 4 (over z), head: 2 (over core), exp: 4 (over y, x).
Axes of the slice: x: 2, y: 2, z: 4, core: 2. Of those that a mesh axis runs over, the one named last changes fastest.
Arguments:
- queries: bfloat16 [16, 64, 32, 128], P('req', 'exp', 'head'), may hold values from -8 to 8
- new_keys: bfloat16 [16, 64, 4, 128], P('req', 'exp', 'head'), may hold values from -8 to 8
- new_values: bfloat16 [16, 64, 4, 128], P('req', 'exp', 'head'), may hold values from -6 to 6
- key_cache: bfloat16 [16, 24576, 4, 128], P('req', 'exp', 'head'), may hold values from -6 to 6
- value_cache: bfloat16 [16, 24576, 4, 128], P('req', 'exp', 'head'), may hold values from -6 to 6
- lengths: int32 [16], P('req'), may hold values from 1 to 24576, 131072 in all
- residual: bfloat16 [1024, 2048], P(('req', 'exp')), may hold values from -24 to 24
- out_weight: bfloat16 [4096, 2048], P('head', 'exp'), may hold values from -1.796875 to 1.796875
- norm_gain: float32 [2048], replicated, may hold values from 0.1 to 1.9
- route_ids: int32 [1024, 8], P(('req', 'exp')), may hold values from 0 to 15, all different within a row; in each aligned block of 64 rows (0 to 63, 64 to 127, ...) at most 64 rows name the same one
- route_weights: float32 [1024, 8], P(('req', 'exp')), may hold values from 0.05 to 0.3
- expert_in: bfloat16 [16, 2048, 2, 768], P(('req', 'exp'), None, None, 'head'), may hold values from -0.125 to 0.125
- expert_out: bfloat16 [16, 768, 2048], P(('req', 'exp'), 'head'), may hold values from -0.21875 to 0.21875
Outputs:
- output: bfloat16 [1024, 2048], P(('req', 'exp'), 'head')
Inputs may be any that keep to these rules, and one draw needn't show every extreme that they name: `route_ids`: each row names 8 different experts. Among the 64 rows of one device (aligned blocks of rows 0 to 63, 64 to 127 and so on) no expert is named by more than 64 rows.
All inputs are finite; a program needn't handle non-finite values. No bound on the sum of `lengths` on one device may be relied on, other than what follows from the above.
Results may differ from a plain program's by a relative error of at most 0.0051.
Values may be sent and summed in bfloat16 or wider, within the bound.
No kernel may reach another device: no remote copies, remote signals or barrier semaphores. Data moves between devices by JAX's collectives and lax.ppermute only.
A program may use at most 192 MiB of HBM per device.

v0:
```python
import functools
import math
import jax
import jax.numpy as jnp
from jax import lax
from jax.experimental import pallas as pl
from jax.experimental.pallas import tpu as pltpu
from jax.sharding import PartitionSpec as P


masked_score = -1e30
norm_epsilon = 1e-06


def attend_kernel(pieces, base, listed, sub, tail, factor, exp_count, info_ref, *refs):
    q_refs = refs[:pieces]
    nk_ref, nv_ref, k_ref, v_ref = refs[pieces : pieces + 4]
    out_refs = refs[pieces + 4 : pieces + 4 + exp_count]
    scratch = refs[pieces + 4 + exp_count :]
    q_all, q_cat, pattern, m_scr, l_scr, acc, p_even, p_odd, stats, turned, staged = scratch
    requests = pl.num_programs(0)
    request = pl.program_id(0)
    head_size = k_ref.shape[2]
    kv = 2
    piece_rows, heads = q_refs[0].shape[1], q_refs[0].shape[2]
    group = heads // kv
    rows = piece_rows * pieces
    lanes = rows * group
    length = info_ref[request + base]
    even_lane = lax.broadcasted_iota(jnp.int32, (lanes, 128), 1) % 2 == 0

    @pl.when(request == 0)
    def _():
        stats[...] = jnp.zeros_like(stats)
        parity = lax.broadcasted_iota(jnp.int32, (16, head_size), 0) % 2
        pattern[0] = (1 - parity).astype(jnp.float32).astype(jnp.bfloat16)
        pattern[1] = parity.astype(jnp.float32).astype(jnp.bfloat16)

    for piece in range(pieces):
        where_to = info_ref[listed + piece] * piece_rows
        q_all[pl.ds(where_to, piece_rows)] = q_refs[piece][0].astype(jnp.float32)
    for head in range(kv):
        chosen = q_all[:, head * group : (head + 1) * group, :].reshape(lanes, head_size)
        q_cat[:, head * head_size : (head + 1) * head_size] = chosen.astype(jnp.bfloat16)

    def spread(block):
        if block.shape[0] < 16:
            left = block * pattern[0, : block.shape[0]]
            right = block * pattern[1, : block.shape[0]]
        else:
            tiles = block.reshape(block.shape[0] // 16, 16, head_size)
            left = (tiles * pattern[0][None]).reshape(block.shape)
            right = (tiles * pattern[1][None]).reshape(block.shape)
        return jnp.concatenate([left, right], axis=1)

    def score(block):
        return lax.dot_general(
            q_cat[...],
            spread(block),
            (((1,), (1,)), ((), ())),
            preferred_element_type=jnp.float32,
        )

    def both_columns(even, odd):
        shape = (lanes, 128)
        return jnp.where(even_lane, jnp.broadcast_to(even, shape), jnp.broadcast_to(odd, shape))

    def reduce_parity(wide, op, neutral):
        even = op(jnp.where(even_lane, wide, neutral), axis=1, keepdims=True)
        odd = op(jnp.where(even_lane, neutral, wide), axis=1, keepdims=True)
        return even, odd

    def init():
        scores = score(nk_ref[0]) * factor
        even = lax.broadcasted_iota(jnp.int32, scores.shape, 1) % 2 == 0
        top_even = jnp.max(jnp.where(even, scores, -jnp.inf), axis=1, keepdims=True)
        top_odd = jnp.max(jnp.where(even, -jnp.inf, scores), axis=1, keepdims=True)
        top_even = top_even.astype(jnp.bfloat16).astype(jnp.float32)
        top_odd = top_odd.astype(jnp.bfloat16).astype(jnp.float32)
        m_scr[...] = both_columns(top_even, top_odd)
        probs = jnp.exp2(
            scores
            - jnp.where(
                even,
                jnp.broadcast_to(top_even, scores.shape),
                jnp.broadcast_to(top_odd, scores.shape),
            )
        )
        l_even = jnp.sum(jnp.where(even, probs, 0.0), axis=1, keepdims=True)
        l_odd = jnp.sum(jnp.where(even, 0.0, probs), axis=1, keepdims=True)
        lane = lax.broadcasted_iota(jnp.int32, (lanes, 128), 1)
        l_scr[...] = jnp.where(lane < 2, both_columns(l_even, l_odd), 0.0)
        acc[...] = jnp.dot(
            probs.astype(jnp.bfloat16), spread(nv_ref[0]), preferred_element_type=jnp.float32
        )

    def piece_of(ref, start, size):
        return ref[0, pl.ds(pl.multiple_of(start * kv, kv * tail), size * kv), :]

    step = 256

    def soften(start, size, target, masked):
        top = m_scr[...]
        total = l_scr[...]
        for tile in range(size * kv // step):
            scores = score(piece_of_tile(k_ref, start, tile))
            for part in range(step // 128):
                piece = scores[:, part * 128 : (part + 1) * 128]
                probs = jnp.exp2(piece * factor - top)
                if masked:
                    lane = lax.broadcasted_iota(jnp.int32, (1, 128), 1)
                    position = start + (tile * step + part * 128 + lane) // kv
                    probs = jnp.where(position < length, probs, 0.0)
                total = total + probs
                at = tile * step + part * 128
                target[:, at : at + 128] = probs.astype(jnp.bfloat16)
        l_scr[...] = total

    def piece_of_tile(ref, start, tile):
        first = pl.multiple_of(start * kv, kv * tail) + tile * step
        return ref[0, pl.ds(first, step), :]

    def weigh(start, size, source):
        values = spread(piece_of(v_ref, start, size))
        acc[...] += jnp.dot(source[:, : size * kv], values, preferred_element_type=jnp.float32)

    init()
    here = length
    pairs = here // (2 * sub)

    def loop(i, carry):
        start = pl.multiple_of(i * 2 * sub, 2 * sub)
        before = jnp.maximum(start - sub, 0)
        soften(start, sub, p_even, False)
        weigh(before, sub, p_odd)
        soften(start + sub, sub, p_odd, False)
        weigh(start, sub, p_even)
        return carry

    p_odd[...] = jnp.zeros_like(p_odd)
    lax.fori_loop(0, pairs, loop, 0)
    weigh(pl.multiple_of(jnp.maximum(pairs * 2 * sub - sub, 0), sub), sub, p_odd)

    def tail_loop(i, carry):
        start = pl.multiple_of(pairs * 2 * sub + i * tail, tail)
        soften(start, tail, p_even, True)
        weigh(start, tail, p_even)
        return carry

    lax.fori_loop(0, (here - pairs * 2 * sub + tail - 1) // tail, tail_loop, 0)
    largest = jnp.max(l_scr[...])

    @pl.when(jnp.logical_not(largest < 1e30))
    def _():
        init()

        def slow_loop(i, carry):
            start = pl.multiple_of(i * tail, tail)
            scores = score(piece_of(k_ref, start, tail)) * factor
            lane = lax.broadcasted_iota(jnp.int32, (1, tail * kv), 1)
            inside = start + lane // kv < length
            scores = jnp.where(inside, scores, masked_score)
            wide = m_scr[...]
            for part in range(tail * kv // 128):
                wide = jnp.maximum(wide, scores[:, part * 128 : (part + 1) * 128])
            even, odd = reduce_parity(wide, jnp.max, -jnp.inf)
            even = even.astype(jnp.bfloat16).astype(jnp.float32)
            odd = odd.astype(jnp.bfloat16).astype(jnp.float32)
            top = both_columns(even, odd)
            fade = jnp.exp2(m_scr[...] - top)
            total = l_scr[...] * fade
            for part in range(tail * kv // 128):
                at = part * 128
                probs = jnp.where(
                    inside[:, at : at + 128], jnp.exp2(scores[:, at : at + 128] - top), 0.0
                )
                total = total + probs
                p_even[:, at : at + 128] = probs.astype(jnp.bfloat16)
            l_scr[...] = total
            m_scr[...] = top
            for head in range(kv):
                columns = slice(head * head_size, (head + 1) * head_size)
                acc[:, columns] = acc[:, columns] * jnp.broadcast_to(
                    fade[:, head : head + 1], (lanes, head_size)
                )
            weigh(start, tail, p_even)
            return carry

        lax.fori_loop(0, (here + tail - 1) // tail, slow_loop, 0)

    share = heads // exp_count
    totals = reduce_parity(l_scr[...], jnp.sum, 0.0)
    lane = lax.broadcasted_iota(jnp.int32, (lanes, head_size), 1)
    member_of_row = lax.broadcasted_iota(jnp.int32, (lanes, head_size), 0) % group
    for head in range(kv):
        total = totals[head]
        inverse = jnp.broadcast_to(1.0 / total, (lanes, head_size))
        columns = slice(head * head_size, (head + 1) * head_size)
        turned[...] = acc[:, columns] * inverse
        upper = total.astype(jnp.bfloat16).astype(jnp.float32)
        kinds = [upper, m_scr[:, head : head + 1], total - upper]
        placed = jnp.zeros((lanes, head_size), jnp.float32)
        for kind, column in enumerate(kinds):
            placed = jnp.where(
                lane == member_of_row + 8 * kind,
                jnp.broadcast_to(column, placed.shape),
                placed,
            )
        gathered = jnp.sum(placed.reshape(rows, group, head_size), axis=1)
        stats[head] = stats[head] + pltpu.roll(gathered, 24 * request, 1)
        for member in range(group):
            index = head * group + member
            target, inside = index // share, index % share
            offset = pl.multiple_of(
                request * (share * head_size) + inside * head_size, head_size
            )
            staged[target, :, pl.ds(offset, head_size)] = turned[
                pl.ds(member, rows, stride=group), :
            ].astype(jnp.bfloat16)

    @pl.when(request == requests - 1)
    def _():
        for target in range(exp_count):
            head = target * share // group
            staged[target, :, requests * share * head_size :] = stats[head].astype(jnp.bfloat16)
        for step_away in range(exp_count):
            out_refs[step_away][...] = staged[info_ref[listed + (-step_away) % exp_count]]


def attend(queries, order, new_keys, new_values, keys, values, local_lengths, base, sub, tail):
    listed, span, kv, head_size = keys.shape
    requests, piece_rows, heads = queries[0].shape[:3]
    pieces = exp_count = len(queries)
    rows = piece_rows * pieces
    share = heads // exp_count
    fresh = new_keys.shape[1]
    width = requests * share * head_size + 128
    info = jnp.concatenate([local_lengths, order])
    factor = head_size ** (-0.5) * math.log2(math.e)
    lanes = rows * heads // kv
    flat = lambda x: x.reshape(listed, x.shape[1] * kv, head_size)
    block = lambda n: pl.BlockSpec((1, n, head_size), lambda r, info: (r + base, 0, 0))
    return pl.pallas_call(
        functools.partial(attend_kernel, pieces, base, listed, sub, tail, factor, exp_count),
        grid_spec=pltpu.PrefetchScalarGridSpec(
            num_scalar_prefetch=1,
            grid=(requests,),
            in_specs=[
                pl.BlockSpec((1, piece_rows, heads, head_size), lambda r, info: (r, 0, 0, 0))
            ]
            * pieces
            + [block(fresh * kv), block(fresh * kv), block(span * kv), block(span * kv)],
            out_specs=[pl.BlockSpec((rows, width), lambda r, info: (0, 0))] * exp_count,
            scratch_shapes=[
                pltpu.VMEM((rows, heads, head_size), jnp.float32),
                pltpu.VMEM((lanes, kv * head_size), jnp.bfloat16),
                pltpu.VMEM((2, 16, head_size), jnp.bfloat16),
                pltpu.VMEM((lanes, 128), jnp.float32),
                pltpu.VMEM((lanes, 128), jnp.float32),
                pltpu.VMEM((lanes, kv * head_size), jnp.float32),
                pltpu.VMEM((lanes, sub * kv), jnp.bfloat16),
                pltpu.VMEM((lanes, sub * kv), jnp.bfloat16),
                pltpu.VMEM((kv, rows, head_size), jnp.float32),
                pltpu.VMEM((lanes, head_size), jnp.float32),
                pltpu.VMEM((exp_count, rows, width), jnp.bfloat16),
            ],
        ),
        out_shape=[jax.ShapeDtypeStruct((rows, width), jnp.bfloat16)] * exp_count,
        compiler_params=pltpu.CompilerParams(dimension_semantics=("arbitrary",)),
        name="attend",
    )(info, *queries, flat(new_keys), flat(new_values), flat(keys), flat(values))


def merge_kernel(parts, batches, share, info_ref, *refs):
    w_refs = refs[batches * parts : (batches + 1) * parts]
    keep_ref, send_ref, attn = refs[(batches + 1) * parts :]
    rows, width = refs[0].shape
    head_size = 128
    requests = (width - head_size) // (share * head_size)
    group_shift = info_ref[0]
    half = info_ref[1]
    for batch in range(batches):
        x_refs = refs[batch * parts : (batch + 1) * parts]
        tables = []
        for x_ref in x_refs:
            table = x_ref[:, width - head_size :].astype(jnp.float32)
            tables.append(pltpu.roll(table, group_shift, 1))
        for request in range(requests):
            first = (batch * requests + request) * rows
            for member in range(share):
                at = 24 * request + member
                tops = [t[:, at + 8 : at + 9] for t in tables]
                sums = [t[:, at : at + 1] + t[:, at + 16 : at + 17] for t in tables]
                top = functools.reduce(jnp.maximum, tops)
                weights = [s * jnp.exp2(m - top) for s, m in zip(sums, tops)]
                inverse = 1.0 / functools.reduce(jnp.add, weights)
                start = (request * share + member) * head_size
                mixed = jnp.zeros((rows, head_size), jnp.float32)
                for weight, x_ref in zip(weights, x_refs):
                    part = x_ref[:, start : start + head_size].astype(jnp.float32)
                    mixed = mixed + jnp.broadcast_to(weight * inverse, part.shape) * part
                attn[
                    first : first + rows, member * head_size : (member + 1) * head_size
                ] = mixed.astype(jnp.bfloat16)
    columns = w_refs[0].shape[1]
    per_half = keep_ref.shape[1] // columns
    for part in range(parts):
        made = jnp.dot(attn[...], w_refs[part][...], preferred_element_type=jnp.float32)
        chunk = info_ref[2 + part]
        inside = pl.multiple_of((chunk % per_half) * columns, columns)

        @pl.when(chunk // per_half == half)
        def _():
            keep_ref[:, pl.ds(inside, columns)] = made

        @pl.when(chunk // per_half != half)
        def _():
            send_ref[:, pl.ds(inside, columns)] = made.astype(jnp.bfloat16)


def merge_project(batches, weights, info, share, requests):
    rows = batches[0][0].shape[0]
    columns = weights[0].shape[1]
    parts = len(weights)
    half_width = parts * columns // 2
    shape = (requests * rows, half_width)
    return pl.pallas_call(
        functools.partial(merge_kernel, parts, len(batches), share),
        in_specs=[pl.BlockSpec(memory_space=pltpu.SMEM)]
        + [pl.BlockSpec(memory_space=pltpu.VMEM)] * ((len(batches) + 1) * parts),
        out_specs=[pl.BlockSpec(memory_space=pltpu.VMEM)] * 2,
        out_shape=[
            jax.ShapeDtypeStruct(shape, jnp.float32),
            jax.ShapeDtypeStruct(shape, jnp.bfloat16),
        ],
        scratch_shapes=[pltpu.VMEM((requests * rows, share * head_size_of(weights, share)), jnp.bfloat16)],
        name="merge_project",
    )(info, *[message for batch in batches for message in batch], *weights)


def head_size_of(weights, share):
    return weights[0].shape[0] // share


def shift(value, axis, step):
    size = lax.axis_size(axis)
    return lax.ppermute(value, axis, [(i, (i + step) % size) for i in range(size)])


def take_block(value, index):
    return lax.dynamic_index_in_dim(value, index, 0, keepdims=False)


def gather_blocks(block, axis):
    return [block] + [shift(block, axis, s) for s in range(1, lax.axis_size(axis))]


def swap(value, axis, bits):
    size = lax.axis_size(axis)
    return lax.ppermute(value, axis, [(i, i ^ bits) for i in range(size)])


def route_table(route_ids, route_weights):
    groups = lax.axis_size("req") * lax.axis_size("exp")
    return jnp.sum(
        jnp.where(
            route_ids[None, :, :] == lax.iota(jnp.int32, groups)[:, None, None],
            route_weights[None, :, :],
            0.0,
        ),
        axis=2,
    )


def exchange_table(column):
    exp_size = lax.axis_size("exp")
    req_at, exp_at = lax.axis_index("req"), lax.axis_index("exp")

    def of(bits):
        picked = lax.dynamic_index_in_dim(
            column, req_at * exp_size + (exp_at ^ bits), 1, keepdims=False
        )
        return picked if bits == 0 else swap(picked, "exp", bits)

    return [of(bits).reshape(-1) for bits in range(exp_size)]


def halves(value, width, axis):
    head_at = lax.axis_index("head")
    own = lax.dynamic_slice_in_dim(value, head_at * width, width, axis)
    other = lax.dynamic_slice_in_dim(value, (1 - head_at) * width, width, axis)
    return own, other


def expert_block(own, weights, gains, maps_in, maps_out):
    other = swap(own, "head", 1)
    wide = [own.astype(jnp.float32), other.astype(jnp.float32)]
    squares = sum(jnp.sum(x * x, axis=-1, keepdims=True) for x in wide)
    factor = lax.rsqrt(squares / (2 * own.shape[1]) + norm_epsilon)
    scaled = [(x * factor * gain).astype(jnp.bfloat16) for x, gain in zip(wide, gains)]
    gate_up = jnp.dot(scaled[0], maps_in[0], preferred_element_type=jnp.float32)
    gate_up = gate_up + jnp.dot(scaled[1], maps_in[1], preferred_element_type=jnp.float32)
    half_units = gate_up.shape[-1] // 2
    activated = (jax.nn.silu(gate_up[:, :half_units]) * gate_up[:, half_units:]).astype(
        jnp.bfloat16
    )
    kept, passed = [
        jnp.dot(activated, maps, preferred_element_type=jnp.float32) * weights[:, None]
        for maps in maps_out
    ]
    return kept, passed.astype(jnp.bfloat16)


def dense_experts(half_hidden, row_weights, gains, maps_in, maps_out):
    row_count, half_width = half_hidden.shape
    req_size = lax.axis_size("req")
    sent = half_hidden.astype(jnp.bfloat16)
    sent, row_weights = lax.optimization_barrier((sent, row_weights))
    column = jnp.concatenate(gather_blocks(sent, "req"), axis=0)
    middle = column.shape[0] // 2

    def run(block, index):
        return expert_block(block, row_weights[index], gains, maps_in, maps_out)

    def whole(kept, passed):
        return kept + swap(passed, "head", 1).astype(jnp.float32)

    def over(value, bits):
        return swap(value.astype(jnp.bfloat16), "exp", bits).astype(jnp.float32)

    near_x = swap(column, "exp", 1)
    near_y = swap(column, "exp", 2)
    own_kept, own_passed = run(column, 0)
    near_x, near_y, own_passed = lax.optimization_barrier((near_x, near_y, own_passed))
    far_top = swap(near_x[:middle], "exp", 2)
    far_low = swap(near_y[middle:], "exp", 1)
    own = whole(own_kept, own_passed)
    for_x = whole(*run(near_x, 1))
    for_y = whole(*run(near_y, 2))
    back_x = over(for_x[:middle], 1)
    back_y = over(for_y[middle:], 2)
    top = own[:middle] + back_x
    low = own[middle:] + back_y
    far = whole(*run(jnp.concatenate([far_top, far_low], axis=0), 3))
    top = top + over(for_y[:middle] + over(far[:middle], 1), 2)
    low = low + over(for_x[middle:] + over(far[middle:], 2), 1)
    plane_sum = jnp.concatenate([top, low], axis=0).reshape(req_size, row_count, half_width)
    mixture = plane_sum[0]
    outgoing = plane_sum.astype(jnp.bfloat16)
    for s in range(1, req_size):
        mixture = mixture + shift(outgoing[s], "req", -s).astype(jnp.float32)
    return mixture


def sparse_experts(half_hidden, route_ids, route_weights, norm_gain, expert_in, expert_out, capacity):
    _, half_width = half_hidden.shape
    head_at = lax.axis_index("head")
    other = shift(half_hidden, "head", 1)
    first = jnp.where(head_at == 0, half_hidden, other)
    second = jnp.where(head_at == 0, other, half_hidden)
    hidden = jnp.concatenate([first, second], axis=1)
    normed = (
        hidden
        * lax.rsqrt(jnp.mean(hidden * hidden, axis=-1, keepdims=True) + norm_epsilon)
        * norm_gain
    ).astype(jnp.bfloat16)
    model_width = 2 * half_width
    local_experts = expert_in.shape[0]
    groups = lax.axis_size("req") * lax.axis_size("exp")
    experts_all = local_experts * groups
    expert_iota = lax.iota(jnp.int32, experts_all)
    named_count = jnp.sum((route_ids[:, :, None] == expert_iota).astype(jnp.int32), axis=1)
    earlier = jnp.cumsum(named_count, axis=0) - named_count
    slot_rank = jnp.take_along_axis(earlier, route_ids, axis=1)
    slot_index = route_ids * capacity + slot_rank
    slot_iota = lax.iota(jnp.int32, experts_all * capacity)
    placing = jnp.any(slot_index[None, :, :] == slot_iota[:, None, None], axis=2).astype(
        jnp.bfloat16
    )
    outgoing = jnp.dot(placing, normed, preferred_element_type=jnp.float32).astype(jnp.bfloat16)
    outgoing = outgoing.reshape(groups, local_experts, capacity, model_width)
    input_maps = expert_in.reshape(local_experts, model_width, -1)
    gate_up = jnp.einsum(
        "geci,eif->gecf",
        lax.all_to_all(outgoing, ("req", "exp"), split_axis=0, concat_axis=0, tiled=True),
        input_maps,
        preferred_element_type=jnp.float32,
    )
    half_units = gate_up.shape[-1] // 2
    activated = (jax.nn.silu(gate_up[..., :half_units]) * gate_up[..., half_units:]).astype(
        jnp.bfloat16
    )
    partial_value = jnp.einsum(
        "gecf,efi->geci", activated, expert_out, preferred_element_type=jnp.float32
    )
    summed = lax.psum_scatter(partial_value, "head", scatter_dimension=3, tiled=True).astype(
        jnp.bfloat16
    )
    returned = lax.all_to_all(summed, ("req", "exp"), split_axis=0, concat_axis=0, tiled=True)
    flat_results = returned.reshape(experts_all * capacity, half_width)
    picked = jnp.take(flat_results, slot_index, axis=0).astype(jnp.float32)
    return jnp.sum(picked * route_weights[:, :, None], axis=1)


def local(
    queries,
    new_keys,
    new_values,
    key_cache,
    value_cache,
    lengths,
    residual,
    out_weight,
    norm_gain,
    route_ids,
    route_weights,
    expert_in,
    expert_out,
):
    requests, span, kv, head_size = key_cache.shape
    heads = queries.shape[2]
    exp_size = lax.axis_size("exp")
    exp_at, head_at = lax.axis_index("exp"), lax.axis_index("head")
    share = heads // exp_size
    group = heads // kv
    sources = (exp_at - lax.iota(jnp.int32, exp_size)) % exp_size
    targets = [(exp_at + s) % exp_size for s in range(exp_size)]

    row_count, model_width = residual.shape
    half_width = model_width // 2
    groups = lax.axis_size("req") * exp_size
    experts_all = expert_in.shape[0] * groups
    capacity = max(2, 2 * row_count * route_ids.shape[1] // experts_all)
    dense = capacity >= row_count and experts_all == groups and exp_size == 4

    batch = requests
    starts = range(0, requests, batch)
    pieces = [
        gather_blocks(lax.slice_in_dim(queries, start, start + batch), "exp") for start in starts
    ]
    local_lengths = jnp.clip(lengths - exp_at * span, 0, span)
    split_weight = out_weight.reshape(exp_size, share * head_size, -1)
    weight_parts = [take_block(split_weight, targets[0])] + [
        shift(take_block(split_weight, targets[s]), "exp", s) for s in range(1, exp_size)
    ]
    if dense:
        column_table = jnp.stack(gather_blocks(route_table(route_ids, route_weights), "req"))
        own_piece, column_table, flat_in = lax.optimization_barrier(
            (pieces[0][0], column_table, expert_in[0].reshape(model_width, -1))
        )
        pieces[0] = [own_piece] + pieces[0][1:]
    received = []
    for start, gathered in zip(starts, pieces):
        messages = attend(
            gathered, sources, new_keys, new_values, key_cache, value_cache, local_lengths,
            start, 512, 256,
        )
        received.append(
            [messages[0]] + [shift(messages[s], "exp", s) for s in range(1, exp_size)]
        )
    if dense:
        maps_in = halves(flat_in, half_width, 0)
        maps_out = halves(expert_out[0], half_width, 1)
        gains = halves(norm_gain, half_width, 0)
        own_message, maps_in, maps_out = lax.optimization_barrier(
            (received[-1][0], maps_in, maps_out)
        )
        received[-1] = [own_message] + received[-1][1:]
    group_shift = (head_size - (exp_at * share) % group) % head_size
    info = jnp.concatenate([jnp.stack([group_shift, head_at]).astype(jnp.int32), sources])
    kept, sent = merge_project(received, weight_parts, info, share, requests)
    if dense:
        kept, column_table = lax.optimization_barrier((kept, column_table))
        row_weights = exchange_table(column_table)
    both = kept + shift(sent, "head", 1).astype(jnp.float32)
    both = both.reshape(exp_size, row_count, half_width)
    outgoing = both.astype(jnp.bfloat16)
    hidden = lax.dynamic_slice_in_dim(residual, head_at * half_width, half_width, 1).astype(
        jnp.float32
    ) + take_block(both, targets[0])
    for s in range(1, exp_size):
        hidden = hidden + shift(take_block(outgoing, targets[s]), "exp", s).astype(jnp.float32)

    if dense:
        mixture = dense_experts(hidden, row_weights, gains, maps_in, maps_out)
    else:
        mixture = sparse_experts(
            hidden, route_ids, route_weights, norm_gain, expert_in, expert_out, capacity
        )
    return (hidden + mixture).astype(jnp.bfloat16)


def solution(mesh):
    return jax.shard_map(
        local,
        mesh=mesh,
        in_specs=(
            P("req", "exp", "head", None),
            P("req", "exp", "head", None),
            P("req", "exp", "head", None),
            P("req", "exp", "head", None),
            P("req", "exp", "head", None),
            P("req"),
            P(("req", "exp"), None),
            P("head", "exp"),
            P(),
            P(("req", "exp"), None),
            P(("req", "exp"), None),
            P(("req", "exp"), None, None, "head"),
            P(("req", "exp"), "head", None),
        ),
        out_specs=P(("req", "exp"), "head"),
        check_vma=False,
    )
```

profile of v0, /device:TPU:0, one launch (start us, length us, event | category | flops | bytes accessed | tf_op | source)
XLA Modules:
  0.0 198.0 jit_solution(8557694601701911906)
XLA Ops:
  0.0 0.7 select_reduce_fusion
  0.7 3.1 %collective-permute-start = (f32[16,64]{1,0:T(8,128)S(1)}, f32[16,64]{1,0:T(8,128)S(1)}, u32[]{:S(2)}, u32[]{:S(2)}) collective-permute-start(f32[16,64]{1,0:T(8,128)S(1)} %select_reduce_fusion), channel_id=1, source_target_pairs={{0,8},{8,16},{16,24},{24,0},{1,9},{9,17},{17,25},{25,1},{2,10},{10... | collective-permute-start | bytes 12296 | tf_op jit(solution)/shard_map/ppermute | solution.py:347
  3.8 2.6 %collective-permute-start.1 = (f32[16,64]{1,0:T(8,128)S(1)}, f32[16,64]{1,0:T(8,128)S(1)}, u32[]{:S(2)}, u32[]{:S(2)}) collective-permute-start(f32[16,64]{1,0:T(8,128)S(1)} %select_reduce_fusion), channel_id=1, source_target_pairs={{0,16},{8,24},{16,0},{24,8},{1,17},{9,25},{17,1},{25,9},{2,18},{10... | collective-permute-start | bytes 12296 | tf_op jit(solution)/shard_map/ppermute | solution.py:347
  6.4 1.3 collective-permute-start.2
  7.8 3.1 %dynamic-slice_bitcast_fusion.2 = (bf16[512,512]{1,0:T(8,128)(2,1)}, bf16[512,512]{1,0:T(8,128)(2,1)}, bf16[512,512]{1,0:T(8,128)(2,1)}, bf16[512,512]{1,0:T(8,128)(2,1)}) fusion(bf16[4,512,512]{2,1,0:T(8,128)(2,1)} %bitcast.75, s32[]{:T(128)S(6)} %select_n.93, s32[]{:T(128)S(6)} %select_n.91, s32[]{:T(128)S(6)} %select_n.89, s32[]{:T(128)S(6)} %select_n.87), kind=kLoop, calls=%fused_computation.96 | loop fusion | bytes 4194320 | tf_op jit(solution)/shard_map/jit(dynamic_index_in_dim)/squeeze | solution.py:351
  10.9 1.5 collective-permute-start.10
  12.4 1.5 collective-permute-start.3
  14.6 1.4 collective-permute-start.5
  16.1 4.2 %copy.16 = bf16[256,8,2,384]{3,1,2,0:T(8,128)(2,1)} copy(bf16[256,8,2,384]{3,2,1,0:T(2,128)(2,1)} %bitcast.74) | data formatting | bytes 6291456
  20.2 1.5 collective-permute-start.11
  21.8 0.8 collective-permute-done.3.refs_1_
  24.4 11.0 %collective-permute-done.4.refs_2_ = bf16[4,16,16,128]{3,2,1,0:T(8,128)(2,1)S(1)} collective-permute-done((bf16[4,16,16,128]{3,2,1,0:T(8,128)(2,1)S(1)}, bf16[4,16,16,128]{3,2,1,0:T(8,128)(2,1)S(1)}, u32[]{:S(2)}, u32[]{:S(2)}) %collective-permute-start.4) | collective-permute-done | bytes 262176 | tf_op jit(solution)/shard_map/ppermute | solution.py:347
  35.4 0.7 copy-done.5
  36.2 39.4 %attend.1 = (bf16[64,2176]{1,0:T(8,128)(2,1)}, bf16[64,2176]{1,0:T(8,128)(2,1)}, bf16[64,2176]{1,0:T(8,128)(2,1)}, bf16[64,2176]{1,0:T(8,128)(2,1)}) custom-call(s32[8]{0:T(128)} %pad_add_fusion.1.info_ref, bf16[4,16,16,128]{3,2,1,0:T(8,128)(2,1)} %refs_0_, bf16[4,16,16,128]{3,2,1,0:T(8,128)(2,1)} %collective-permute-done.3.refs_1_, ...), custom_call_target="tpu_custom_call" | custom-call | tf_op jit(solution)/shard_map/attend/pallas_call | solution.py:243
  75.7 2.8 %collective-permute-start.8 = (bf16[64,2176]{1,0:T(8,128)(2,1)}, bf16[64,2176]{1,0:T(8,128)(2,1)}, u32[]{:S(2)}, u32[]{:S(2)}) collective-permute-start(bf16[64,2176]{1,0:T(8,128)(2,1)} %get-tuple-element.35), channel_id=1, source_target_pairs={{0,3},{1,0},{2,1},{3,2},{4,7},{5,4},{6,5},{7,6},{8,11},{9,8},{10,9... | collective-permute-start | bytes 835592 | tf_op jit(solution)/shard_map/ppermute | solution.py:347
  79.1 3.2 %constant_dynamic-slice_fusion.4 = (bf16[1024,768]{1,0:T(8,128)(2,1)}, bf16[1024,768]{1,0:T(8,128)(2,1)S(1)}) fusion(bf16[2048,768]{1,0:T(8,128)(2,1)} %bitcast.71, s32[]{:T(128)S(6)} %select_n.85, s32[]{:T(128)S(6)} %select_n.80), kind=kLoop, calls=%fused_computation.134 | loop fusion | bytes 6291464 | tf_op jit(solution)/shard_map/dynamic_slice | solution.py:391
  82.4 3.9 %collective-permute-done.6.refs_1_ = bf16[64,2176]{1,0:T(8,128)(2,1)S(1)} collective-permute-done((bf16[64,2176]{1,0:T(8,128)(2,1)}, bf16[64,2176]{1,0:T(8,128)(2,1)S(1)}, u32[]{:S(2)}, u32[]{:S(2)}) %collective-permute-start.6) | collective-permute-done | bytes 278560 | tf_op jit(solution)/shard_map/ppermute | solution.py:347
  86.2 2.3 %collective-permute-done.7.refs_2_ = bf16[64,2176]{1,0:T(8,128)(2,1)} collective-permute-done((bf16[64,2176]{1,0:T(8,128)(2,1)}, bf16[64,2176]{1,0:T(8,128)(2,1)}, u32[]{:S(2)}, u32[]{:S(2)}) %collective-permute-start.7) | collective-permute-done | bytes 278560 | tf_op jit(solution)/shard_map/ppermute | solution.py:347
  88.5 5.1 %merge_project.1 = (f32[256,1024]{1,0:T(8,128)}, bf16[256,1024]{1,0:T(8,128)(2,1)}) custom-call(s32[6]{0:T(128)} %pad_add_fusion.info_ref, bf16[64,2176]{1,0:T(8,128)(2,1)} %get-tuple-element.32.refs_0_, bf16[64,2176]{1,0:T(8,128)(2,1)} %copy-done.3, bf16[64,2176]{1,0:T(8,128)(2,1)} %collective-permute-done.7.refs_2_, ...), custom_call_target="tpu_custom_call" | custom-call | tf_op jit(solution)/shard_map/merge_project/pallas_call | solution.py:327
  93.6 2.1 %collective-permute-done.12 = bf16[256,1024]{1,0:T(8,128)(2,1)S(1)} collective-permute-done((bf16[256,1024]{1,0:T(8,128)(2,1)}, bf16[256,1024]{1,0:T(8,128)(2,1)S(1)}, u32[]{:S(2)}, u32[]{:S(2)}) %collective-permute-start.12) | collective-permute-done | bytes 524320 | tf_op jit(solution)/shard_map/ppermute | solution.py:347
  95.7 1.4 convert_add_fusion.3
  97.1 1.0 copy-done.1
  98.2 1.4 collective-permute-start.13
  99.6 1.8 collective-permute-start.14
  101.4 1.2 collective-permute-start.15
  102.6 1.5 constant_dynamic-slice_fusion
  104.1 0.8 collective-permute-start.16
  105.1 2.5 %collective-permute-done.16 = f32[4,64]{1,0:T(4,128)S(1)} collective-permute-done((f32[4,64]{1,0:T(4,128)S(1)}, f32[4,64]{1,0:T(4,128)S(1)}, u32[]{:S(2)}, u32[]{:S(2)}) %collective-permute-start.16) | collective-permute-done | bytes 1056 | tf_op jit(solution)/shard_map/ppermute | solution.py:360
  107.7 1.6 collective-permute-start.18
  109.3 0.8 reshape.106
  110.1 0.8 reshape.107
  110.8 1.6 collective-permute-done.18
  112.5 0.8 reshape.108
  113.2 1.4 fusion.82
  114.6 6.7 %collective-permute-start.19 = (bf16[64,1024]{1,0:T(8,128)(2,1)S(1)}, bf16[64,1024]{1,0:T(8,128)(2,1)S(1)}, u32[]{:S(2)}, u32[]{:S(2)}) collective-permute-start(bf16[64,1024]{1,0:T(8,128)(2,1)S(1)} %get-tuple-element.41), channel_id=1, source_target_pairs={{0,8},{8,16},{16,24},{24,0},{1,9},{9,17},{17,25},{25,1},{2,10},{10... | collective-permute-start | bytes 393224 | tf_op jit(solution)/shard_map/ppermute | solution.py:347
  121.3 2.7 %collective-permute-start.21 = (bf16[64,1024]{1,0:T(8,128)(2,1)S(1)}, bf16[64,1024]{1,0:T(8,128)(2,1)S(1)}, u32[]{:S(2)}, u32[]{:S(2)}) collective-permute-start(bf16[64,1024]{1,0:T(8,128)(2,1)S(1)} %get-tuple-element.41), channel_id=1, source_target_pairs={{0,24},{8,0},{16,8},{24,16},{1,25},{9,1},{17,9},{25,17},{2,26},{10... | collective-permute-start | bytes 393224 | tf_op jit(solution)/shard_map/ppermute | solution.py:347
  124.0 1.2 collective-permute-done.19
  125.2 4.2 %collective-permute-done.20 = bf16[64,1024]{1,0:T(8,128)(2,1)S(1)} collective-permute-done((bf16[64,1024]{1,0:T(8,128)(2,1)S(1)}, bf16[64,1024]{1,0:T(8,128)(2,1)S(1)}, u32[]{:S(2)}, u32[]{:S(2)}) %collective-permute-start.20) | collective-permute-done | bytes 131104 | tf_op jit(solution)/shard_map/ppermute | solution.py:347
  129.5 0.7 fusion.86
  130.8 1.7 collective-permute-start.24
  133.5 0.6 fusion.45
  134.8 9.8 %collective-permute-done.23 = bf16[256,1024]{1,0:T(8,128)(2,1)S(1)} collective-permute-done((bf16[256,1024]{1,0:T(8,128)(2,1)S(1)}, bf16[256,1024]{1,0:T(8,128)(2,1)S(1)}, u32[]{:S(2)}, u32[]{:S(2)}) %collective-permute-start.23) | collective-permute-done | bytes 524320 | tf_op jit(solution)/shard_map/ppermute | solution.py:360
  144.9 1.8 collective-permute-start.31
  147.9 4.6 %collective-permute-done.31 = bf16[128,1024]{1,0:T(8,128)(2,1)S(1)} collective-permute-done((bf16[128,1024]{1,0:T(8,128)(2,1)S(1)}, bf16[128,1024]{1,0:T(8,128)(2,1)S(1)}, u32[]{:S(2)}, u32[]{:S(2)}) %collective-permute-start.31) | collective-permute-done | bytes 262176 | tf_op jit(solution)/shard_map/ppermute | solution.py:360
  152.5 3.0 %collective-permute-done.32 = bf16[128,1024]{1,0:T(8,128)(2,1)S(1)} collective-permute-done((bf16[128,1024]{1,0:T(8,128)(2,1)S(1)}, bf16[128,1024]{1,0:T(8,128)(2,1)S(1)}, u32[]{:S(2)}, u32[]{:S(2)}) %collective-permute-start.32) | collective-permute-done | bytes 262176 | tf_op jit(solution)/shard_map/ppermute | solution.py:360
  156.0 0.6 fusion.36
  156.7 0.6 convolution_add_fusion
  158.6 0.6 fusion.39
  159.3 0.6 convolution_add_fusion.1
  160.2 0.6 fusion.28
  160.9 0.6 fusion.32
  164.5 1.5 collective-permute-start.35
  167.2 1.7 collective-permute-start.28
  168.9 4.9 %collective-permute-done.35 = bf16[128,1024]{1,0:T(8,128)(2,1)S(1)} collective-permute-done((bf16[128,1024]{1,0:T(8,128)(2,1)S(1)}, bf16[128,1024]{1,0:T(8,128)(2,1)S(1)}, u32[]{:S(2)}, u32[]{:S(2)}) %collective-permute-start.35) | collective-permute-done | bytes 262176 | tf_op jit(solution)/shard_map/ppermute | solution.py:360
  173.9 1.8 collective-permute-start.36
  175.6 2.9 %collective-permute-done.39 = bf16[128,1024]{1,0:T(8,128)(2,1)S(1)} collective-permute-done((bf16[128,1024]{1,0:T(8,128)(2,1)S(1)}, bf16[128,1024]{1,0:T(8,128)(2,1)S(1)}, u32[]{:S(2)}, u32[]{:S(2)}) %collective-permute-start.39) | collective-permute-done | bytes 262176 | tf_op jit(solution)/shard_map/ppermute | solution.py:360
  179.5 3.7 %collective-permute-done.36 = bf16[128,1024]{1,0:T(8,128)(2,1)S(1)} collective-permute-done((bf16[128,1024]{1,0:T(8,128)(2,1)S(1)}, bf16[128,1024]{1,0:T(8,128)(2,1)S(1)}, u32[]{:S(2)}, u32[]{:S(2)}) %collective-permute-start.36) | collective-permute-done | bytes 262176 | tf_op jit(solution)/shard_map/ppermute | solution.py:360
  183.2 1.9 collective-permute-done.40
  185.4 2.2 %collective-permute-start.41 = (bf16[64,1024]{1,0:T(8,128)(2,1)S(1)}, bf16[64,1024]{1,0:T(8,128)(2,1)S(1)}, u32[]{:S(2)}, u32[]{:S(2)}) collective-permute-start(bf16[64,1024]{1,0:T(8,128)(2,1)S(1)} %get-tuple-element.70), channel_id=1, source_target_pairs={{0,16},{8,24},{16,0},{24,8},{1,17},{9,25},{17,1},{25,9},{2,18},{10... | collective-permute-start | bytes 393224 | tf_op jit(solution)/shard_map/ppermute | solution.py:347
  187.6 2.8 %collective-permute-start.42 = (bf16[64,1024]{1,0:T(8,128)(2,1)S(1)}, bf16[64,1024]{1,0:T(8,128)(2,1)S(1)}, u32[]{:S(2)}, u32[]{:S(2)}) collective-permute-start(bf16[64,1024]{1,0:T(8,128)(2,1)S(1)} %get-tuple-element.71), channel_id=1, source_target_pairs={{0,8},{8,16},{16,24},{24,0},{1,9},{9,17},{17,25},{25,1},{2,10},{10... | collective-permute-start | bytes 393224 | tf_op jit(solution)/shard_map/ppermute | solution.py:347
  190.4 1.0 collective-permute-start.37
  191.5 5.0 %collective-permute-done.41 = bf16[64,1024]{1,0:T(8,128)(2,1)S(1)} collective-permute-done((bf16[64,1024]{1,0:T(8,128)(2,1)S(1)}, bf16[64,1024]{1,0:T(8,128)(2,1)S(1)}, u32[]{:S(2)}, u32[]{:S(2)}) %collective-permute-start.41) | collective-permute-done | bytes 131104 | tf_op jit(solution)/shard_map/ppermute | solution.py:347
  196.5 0.7 collective-permute-done.37
  197.2 0.7 fusion.76
  (110 shorter events, 15.0 us)
Async XLA Ops:
  0.7 13.3 %collective-permute-start = (f32[16,64]{1,0:T(8,128)S(1)}, f32[16,64]{1,0:T(8,128)S(1)}, u32[]{:S(2)}, u32[]{:S(2)}) collective-permute-start(f32[16,64]{1,0:T(8,128)S(1)} %select_reduce_fusion), channel_id=1, source_target_pairs={{0,8},{8,16},{16,24},{24,0},{1,9},{9,17},{17,25},{25,1},{2,10},{10... | collective-permute-start | bytes 12296 | tf_op jit(solution)/shard_map/ppermute | solution.py:347
  3.8 10.8 %collective-permute-start.1 = (f32[16,64]{1,0:T(8,128)S(1)}, f32[16,64]{1,0:T(8,128)S(1)}, u32[]{:S(2)}, u32[]{:S(2)}) collective-permute-start(f32[16,64]{1,0:T(8,128)S(1)} %select_reduce_fusion), channel_id=1, source_target_pairs={{0,16},{8,24},{16,0},{24,8},{1,17},{9,25},{17,1},{25,9},{2,18},{10... | collective-permute-start | bytes 12296 | tf_op jit(solution)/shard_map/ppermute | solution.py:347
  6.4 13.8 %collective-permute-start.2 = (f32[16,64]{1,0:T(8,128)S(1)}, f32[16,64]{1,0:T(8,128)S(1)}, u32[]{:S(2)}, u32[]{:S(2)}) collective-permute-start(f32[16,64]{1,0:T(8,128)S(1)} %select_reduce_fusion), channel_id=1, source_target_pairs={{0,24},{8,0},{16,8},{24,16},{1,25},{9,1},{17,9},{25,17},{2,26},{10... | collective-permute-start | bytes 12296 | tf_op jit(solution)/shard_map/ppermute | solution.py:347
  7.8 4.6 %copy-start.4 = (bf16[4,16,16,128]{3,2,1,0:T(8,128)(2,1)S(1)}, bf16[4,16,16,128]{3,2,1,0:T(8,128)(2,1)}, u32[]{:S(2)}) copy-start(bf16[4,16,16,128]{3,2,1,0:T(8,128)(2,1)} %refs_0_) | copy-start | bytes 786436
  7.8 6.1 %copy-start.8 = (s32[4]{0:T(128)S(1)}, s32[4]{0:T(128)}, u32[]{:S(2)}) copy-start(s32[4]{0:T(128)} %param.18) | copy-start | bytes 52
  7.8 6.1 %copy-start.2 = (bf16[1,384,2048]{2,1,0:T(8,128)(2,1)S(1)}, bf16[1,384,2048]{2,1,0:T(8,128)(2,1)}, u32[]{:S(2)}) copy-start(bf16[1,384,2048]{2,1,0:T(8,128)(2,1)} %param.25) | copy-start | bytes 4718596
  10.9 64.8 %collective-permute-start.10 = (bf16[512,512]{1,0:T(8,128)(2,1)}, bf16[512,512]{1,0:T(8,128)(2,1)}, u32[]{:S(2)}, u32[]{:S(2)}) collective-permute-start(bf16[512,512]{1,0:T(8,128)(2,1)} %get-tuple-element.58), channel_id=1, source_target_pairs={{0,2},{1,3},{2,0},{3,1},{4,6},{5,7},{6,4},{7,5},{8,10},{9,11},{10,... | collective-permute-start | bytes 1572872 | tf_op jit(solution)/shard_map/ppermute | solution.py:347
  12.4 10.2 %collective-permute-start.3 = (bf16[4,16,16,128]{3,2,1,0:T(8,128)(2,1)S(1)}, bf16[4,16,16,128]{3,2,1,0:T(8,128)(2,1)}, u32[]{:S(2)}, u32[]{:S(2)}) collective-permute-start(bf16[4,16,16,128]{3,2,1,0:T(8,128)(2,1)S(1)} %copy-done.4), channel_id=1, source_target_pairs={{0,1},{1,2},{2,3},{3,0},{4,5},{5,6},{6,7},{7,4},{8,9},{9,10},{10,1... | collective-permute-start | bytes 786440 | tf_op jit(solution)/shard_map/ppermute | solution.py:347
  14.0 21.3 %collective-permute-start.4 = (bf16[4,16,16,128]{3,2,1,0:T(8,128)(2,1)S(1)}, bf16[4,16,16,128]{3,2,1,0:T(8,128)(2,1)S(1)}, u32[]{:S(2)}, u32[]{:S(2)}) collective-permute-start(bf16[4,16,16,128]{3,2,1,0:T(8,128)(2,1)S(1)} %copy-done.4), channel_id=1, source_target_pairs={{0,2},{1,3},{2,0},{3,1},{4,6},{5,7},{6,4},{7,5},{8,10},{9,11},{10,... | collective-permute-start | bytes 786440 | tf_op jit(solution)/shard_map/ppermute | solution.py:347
  14.6 20.7 %collective-permute-start.5 = (bf16[4,16,16,128]{3,2,1,0:T(8,128)(2,1)S(1)}, bf16[4,16,16,128]{3,2,1,0:T(8,128)(2,1)S(1)}, u32[]{:S(2)}, u32[]{:S(2)}) collective-permute-start(bf16[4,16,16,128]{3,2,1,0:T(8,128)(2,1)S(1)} %copy-done.4), channel_id=1, source_target_pairs={{0,3},{1,0},{2,1},{3,2},{4,7},{5,4},{6,5},{7,6},{8,11},{9,8},{10,9... | collective-permute-start | bytes 786440 | tf_op jit(solution)/shard_map/ppermute | solution.py:347
  20.2 62.2 %collective-permute-start.11 = (bf16[512,512]{1,0:T(8,128)(2,1)}, bf16[512,512]{1,0:T(8,128)(2,1)}, u32[]{:S(2)}, u32[]{:S(2)}) collective-permute-start(bf16[512,512]{1,0:T(8,128)(2,1)} %get-tuple-element.57), channel_id=1, source_target_pairs={{0,3},{1,0},{2,1},{3,2},{4,7},{5,4},{6,5},{7,6},{8,11},{9,8},{10,9... | collective-permute-start | bytes 1572872 | tf_op jit(solution)/shard_map/ppermute | solution.py:347
  22.6 59.8 %collective-permute-start.9 = (bf16[512,512]{1,0:T(8,128)(2,1)}, bf16[512,512]{1,0:T(8,128)(2,1)}, u32[]{:S(2)}, u32[]{:S(2)}) collective-permute-start(bf16[512,512]{1,0:T(8,128)(2,1)} %get-tuple-element.59), channel_id=1, source_target_pairs={{0,1},{1,2},{2,3},{3,0},{4,5},{5,6},{6,7},{7,4},{8,9},{9,10},{10,1... | collective-permute-start | bytes 1572872 | tf_op jit(solution)/shard_map/ppermute | solution.py:347
  35.4 0.7 copy-start.5
  35.4 0.8 copy-start.6
  75.6 10.6 %collective-permute-start.6 = (bf16[64,2176]{1,0:T(8,128)(2,1)}, bf16[64,2176]{1,0:T(8,128)(2,1)S(1)}, u32[]{:S(2)}, u32[]{:S(2)}) collective-permute-start(bf16[64,2176]{1,0:T(8,128)(2,1)} %get-tuple-element.33), channel_id=1, source_target_pairs={{0,1},{1,2},{2,3},{3,0},{4,5},{5,6},{6,7},{7,4},{8,9},{9,10},{10,1... | collective-permute-start | bytes 835592 | tf_op jit(solution)/shard_map/ppermute | solution.py:347
  75.6 12.9 %collective-permute-start.7 = (bf16[64,2176]{1,0:T(8,128)(2,1)}, bf16[64,2176]{1,0:T(8,128)(2,1)}, u32[]{:S(2)}, u32[]{:S(2)}) collective-permute-start(bf16[64,2176]{1,0:T(8,128)(2,1)} %get-tuple-element.34), channel_id=1, source_target_pairs={{0,2},{1,3},{2,0},{3,1},{4,6},{5,7},{6,4},{7,5},{8,10},{9,11},{10,... | collective-permute-start | bytes 835592 | tf_op jit(solution)/shard_map/ppermute | solution.py:347
  75.7 12.8 %collective-permute-start.8 = (bf16[64,2176]{1,0:T(8,128)(2,1)}, bf16[64,2176]{1,0:T(8,128)(2,1)}, u32[]{:S(2)}, u32[]{:S(2)}) collective-permute-start(bf16[64,2176]{1,0:T(8,128)(2,1)} %get-tuple-element.35), channel_id=1, source_target_pairs={{0,3},{1,0},{2,1},{3,2},{4,7},{5,4},{6,5},{7,6},{8,11},{9,8},{10,9... | collective-permute-start | bytes 835592 | tf_op jit(solution)/shard_map/ppermute | solution.py:347
  86.2 2.3 %copy-start.3 = (bf16[64,2176]{1,0:T(8,128)(2,1)}, bf16[64,2176]{1,0:T(8,128)(2,1)S(1)}, u32[]{:S(2)}) copy-start(bf16[64,2176]{1,0:T(8,128)(2,1)S(1)} %collective-permute-done.6.refs_1_) | copy-start | bytes 835588
  93.6 2.1 %collective-permute-start.12 = (bf16[256,1024]{1,0:T(8,128)(2,1)}, bf16[256,1024]{1,0:T(8,128)(2,1)S(1)}, u32[]{:S(2)}, u32[]{:S(2)}) collective-permute-start(bf16[256,1024]{1,0:T(8,128)(2,1)} %get-tuple-element.39), channel_id=1, source_target_pairs={{0,4},{4,0},{1,5},{5,1},{2,6},{6,2},{3,7},{7,3},{8,12},{12,8},{9,1... | collective-permute-start | bytes 1572872 | tf_op jit(solution)/shard_map/ppermute | solution.py:347
  97.1 1.0 copy-start.1
  98.2 15.0 %collective-permute-start.13 = (bf16[64,1024]{1,0:T(8,128)(2,1)S(1)}, bf16[64,1024]{1,0:T(8,128)(2,1)}, u32[]{:S(2)}, u32[]{:S(2)}) collective-permute-start(bf16[64,1024]{1,0:T(8,128)(2,1)S(1)} %get-tuple-element.67), channel_id=1, source_target_pairs={{0,1},{1,2},{2,3},{3,0},{4,5},{5,6},{6,7},{7,4},{8,9},{9,10},{10,1... | collective-permute-start | bytes 393224 | tf_op jit(solution)/shard_map/ppermute | solution.py:347
  99.6 13.6 %collective-permute-start.14 = (bf16[64,1024]{1,0:T(8,128)(2,1)S(1)}, bf16[64,1024]{1,0:T(8,128)(2,1)}, u32[]{:S(2)}, u32[]{:S(2)}) collective-permute-start(bf16[64,1024]{1,0:T(8,128)(2,1)S(1)} %get-tuple-element.69), channel_id=1, source_target_pairs={{0,2},{1,3},{2,0},{3,1},{4,6},{5,7},{6,4},{7,5},{8,10},{9,11},{10,... | collective-permute-start | bytes 393224 | tf_op jit(solution)/shard_map/ppermute | solution.py:347
  101.4 11.8 %collective-permute-start.15 = (bf16[64,1024]{1,0:T(8,128)(2,1)S(1)}, bf16[64,1024]{1,0:T(8,128)(2,1)}, u32[]{:S(2)}, u32[]{:S(2)}) collective-permute-start(bf16[64,1024]{1,0:T(8,128)(2,1)S(1)} %get-tuple-element.68), channel_id=1, source_target_pairs={{0,3},{1,0},{2,1},{3,2},{4,7},{5,4},{6,5},{7,6},{8,11},{9,8},{10,9... | collective-permute-start | bytes 393224 | tf_op jit(solution)/shard_map/ppermute | solution.py:347
  104.1 3.6 %collective-permute-start.16 = (f32[4,64]{1,0:T(4,128)S(1)}, f32[4,64]{1,0:T(4,128)S(1)}, u32[]{:S(2)}, u32[]{:S(2)}) collective-permute-start(f32[4,64]{1,0:T(4,128)S(1)} %bitcast.83), channel_id=1, source_target_pairs={{0,1},{1,0},{2,3},{3,2},{4,5},{5,4},{6,7},{7,6},{8,9},{9,8},{10,11... | collective-permute-start | bytes 3080 | tf_op jit(solution)/shard_map/ppermute | solution.py:360
  104.9 5.2 %collective-permute-start.17 = (f32[4,64]{1,0:T(4,128)S(1)}, f32[4,64]{1,0:T(4,128)}, u32[]{:S(2)}, u32[]{:S(2)}) collective-permute-start(f32[4,64]{1,0:T(4,128)S(1)} %bitcast.82), channel_id=1, source_target_pairs={{0,2},{1,3},{2,0},{3,1},{4,6},{5,7},{6,4},{7,5},{8,10},{9,11},{10,... | collective-permute-start | bytes 3080 | tf_op jit(solution)/shard_map/ppermute | solution.py:360
  107.7 1.6 copy-start.7
  107.7 4.8 %collective-permute-start.18 = (f32[4,64]{1,0:T(4,128)}, f32[4,64]{1,0:T(4,128)}, u32[]{:S(2)}, u32[]{:S(2)}) collective-permute-start(f32[4,64]{1,0:T(4,128)} %bitcast.24), channel_id=1, source_target_pairs={{0,3},{1,2},{2,1},{3,0},{4,7},{5,6},{6,5},{7,4},{8,11},{9,10},{10,... | collective-permute-start | bytes 3080 | tf_op jit(solution)/shard_map/ppermute | solution.py:360
  113.2 19.7 %copy-start = (bf16[1024,768]{1,0:T(8,128)(2,1)S(1)}, bf16[1024,768]{1,0:T(8,128)(2,1)}, u32[]{:S(2)}) copy-start(bf16[1024,768]{1,0:T(8,128)(2,1)} %get-tuple-element.43) | copy-start | bytes 4718596
  114.6 10.6 %collective-permute-start.19 = (bf16[64,1024]{1,0:T(8,128)(2,1)S(1)}, bf16[64,1024]{1,0:T(8,128)(2,1)S(1)}, u32[]{:S(2)}, u32[]{:S(2)}) collective-permute-start(bf16[64,1024]{1,0:T(8,128)(2,1)S(1)} %get-tuple-element.41), channel_id=1, source_target_pairs={{0,8},{8,16},{16,24},{24,0},{1,9},{9,17},{17,25},{25,1},{2,10},{10... | collective-permute-start | bytes 393224 | tf_op jit(solution)/shard_map/ppermute | solution.py:347
  121.3 8.1 %collective-permute-start.20 = (bf16[64,1024]{1,0:T(8,128)(2,1)S(1)}, bf16[64,1024]{1,0:T(8,128)(2,1)S(1)}, u32[]{:S(2)}, u32[]{:S(2)}) collective-permute-start(bf16[64,1024]{1,0:T(8,128)(2,1)S(1)} %get-tuple-element.41), channel_id=1, source_target_pairs={{0,16},{8,24},{16,0},{24,8},{1,17},{9,25},{17,1},{25,9},{2,18},{10... | collective-permute-start | bytes 393224 | tf_op jit(solution)/shard_map/ppermute | solution.py:347
  121.3 8.1 %collective-permute-start.21 = (bf16[64,1024]{1,0:T(8,128)(2,1)S(1)}, bf16[64,1024]{1,0:T(8,128)(2,1)S(1)}, u32[]{:S(2)}, u32[]{:S(2)}) collective-permute-start(bf16[64,1024]{1,0:T(8,128)(2,1)S(1)} %get-tuple-element.41), channel_id=1, source_target_pairs={{0,24},{8,0},{16,8},{24,16},{1,25},{9,1},{17,9},{25,17},{2,26},{10... | collective-permute-start | bytes 393224 | tf_op jit(solution)/shard_map/ppermute | solution.py:347
  129.5 3.2 %collective-permute-start.22 = (bf16[256,1024]{1,0:T(8,128)(2,1)S(1)}, bf16[256,1024]{1,0:T(8,128)(2,1)S(1)}, u32[]{:S(2)}, u32[]{:S(2)}) collective-permute-start(bf16[256,1024]{1,0:T(8,128)(2,1)S(1)} %constant_dynamic-update-slice_fusion), channel_id=1, source_target_pairs={{0,4},{4,0},{1,5},{5,1},{2,6},{6,2},{3,7},{7,3},{8,12},{12,8},{9,1... | collective-permute-start | bytes 1572872 | tf_op jit(solution)/shard_map/ppermute | solution.py:360
  130.3 14.3 %collective-permute-start.23 = (bf16[256,1024]{1,0:T(8,128)(2,1)S(1)}, bf16[256,1024]{1,0:T(8,128)(2,1)S(1)}, u32[]{:S(2)}, u32[]{:S(2)}) collective-permute-start(bf16[256,1024]{1,0:T(8,128)(2,1)S(1)} %constant_dynamic-update-slice_fusion), channel_id=1, source_target_pairs={{0,1},{1,0},{2,3},{3,2},{4,5},{5,4},{6,7},{7,6},{8,9},{9,8},{10,11... | collective-permute-start | bytes 1572872 | tf_op jit(solution)/shard_map/ppermute | solution.py:360
  130.8 14.0 %collective-permute-start.24 = (bf16[256,1024]{1,0:T(8,128)(2,1)S(1)}, bf16[256,1024]{1,0:T(8,128)(2,1)S(1)}, u32[]{:S(2)}, u32[]{:S(2)}) collective-permute-start(bf16[256,1024]{1,0:T(8,128)(2,1)S(1)} %constant_dynamic-update-slice_fusion), channel_id=1, source_target_pairs={{0,2},{1,3},{2,0},{3,1},{4,6},{5,7},{6,4},{7,5},{8,10},{9,11},{10,... | collective-permute-start | bytes 1572872 | tf_op jit(solution)/shard_map/ppermute | solution.py:360
  144.9 7.6 %collective-permute-start.31 = (bf16[128,1024]{1,0:T(8,128)(2,1)S(1)}, bf16[128,1024]{1,0:T(8,128)(2,1)S(1)}, u32[]{:S(2)}, u32[]{:S(2)}) collective-permute-start(bf16[128,1024]{1,0:T(8,128)(2,1)S(1)} %slice.87), channel_id=1, source_target_pairs={{0,2},{1,3},{2,0},{3,1},{4,6},{5,7},{6,4},{7,5},{8,10},{9,11},{10,... | collective-permute-start | bytes 786440 | tf_op jit(solution)/shard_map/ppermute | solution.py:360
  146.6 9.2 %collective-permute-start.29 = (bf16[256,1024]{1,0:T(8,128)(2,1)S(1)}, bf16[256,1024]{1,0:T(8,128)(2,1)S(1)}, u32[]{:S(2)}, u32[]{:S(2)}) collective-permute-start(bf16[256,1024]{1,0:T(8,128)(2,1)S(1)} %collective-permute-done.24), channel_id=1, source_target_pairs={{0,4},{4,0},{1,5},{5,1},{2,6},{6,2},{3,7},{7,3},{8,12},{12,8},{9,1... | collective-permute-start | bytes 1572872 | tf_op jit(solution)/shard_map/ppermute | solution.py:360
  146.7 11.8 %collective-permute-start.26 = (bf16[256,1024]{1,0:T(8,128)(2,1)S(1)}, bf16[256,1024]{1,0:T(8,128)(2,1)S(1)}, u32[]{:S(2)}, u32[]{:S(2)}) collective-permute-start(bf16[256,1024]{1,0:T(8,128)(2,1)S(1)} %collective-permute-done.23), channel_id=1, source_target_pairs={{0,4},{4,0},{1,5},{5,1},{2,6},{6,2},{3,7},{7,3},{8,12},{12,8},{9,1... | collective-permute-start | bytes 1572872 | tf_op jit(solution)/shard_map/ppermute | solution.py:360
  147.2 8.3 %collective-permute-start.32 = (bf16[128,1024]{1,0:T(8,128)(2,1)S(1)}, bf16[128,1024]{1,0:T(8,128)(2,1)S(1)}, u32[]{:S(2)}, u32[]{:S(2)}) collective-permute-start(bf16[128,1024]{1,0:T(8,128)(2,1)S(1)} %slice.88), channel_id=1, source_target_pairs={{0,1},{1,0},{2,3},{3,2},{4,5},{5,4},{6,7},{7,6},{8,9},{9,8},{10,11... | collective-permute-start | bytes 786440 | tf_op jit(solution)/shard_map/ppermute | solution.py:360
  147.6 31.4 %collective-permute-start.25 = (bf16[256,1024]{1,0:T(8,128)(2,1)S(1)}, bf16[256,1024]{1,0:T(8,128)(2,1)S(1)}, u32[]{:S(2)}, u32[]{:S(2)}) collective-permute-start(bf16[256,1024]{1,0:T(8,128)(2,1)S(1)} %fusion), channel_id=1, source_target_pairs={{0,4},{4,0},{1,5},{5,1},{2,6},{6,2},{3,7},{7,3},{8,12},{12,8},{9,1... | collective-permute-start | bytes 1572872 | tf_op jit(solution)/shard_map/ppermute | solution.py:360
  155.6 4.5 %collective-permute-start.33 = (bf16[256,1024]{1,0:T(8,128)(2,1)S(1)}, bf16[256,1024]{1,0:T(8,128)(2,1)S(1)}, u32[]{:S(2)}, u32[]{:S(2)}) collective-permute-start(bf16[256,1024]{1,0:T(8,128)(2,1)S(1)} %constant_dynamic-update-slice_fusion.4), channel_id=1, source_target_pairs={{0,4},{4,0},{1,5},{5,1},{2,6},{6,2},{3,7},{7,3},{8,12},{12,8},{9,1... | collective-permute-start | bytes 1572872 | tf_op jit(solution)/shard_map/ppermute | solution.py:360
  157.9 5.3 %collective-permute-start.30 = (bf16[256,1024]{1,0:T(8,128)(2,1)S(1)}, bf16[256,1024]{1,0:T(8,128)(2,1)S(1)}, u32[]{:S(2)}, u32[]{:S(2)}) collective-permute-start(bf16[256,1024]{1,0:T(8,128)(2,1)S(1)} %fusion.2), channel_id=1, source_target_pairs={{0,4},{4,0},{1,5},{5,1},{2,6},{6,2},{3,7},{7,3},{8,12},{12,8},{9,1... | collective-permute-start | bytes 1572872 | tf_op jit(solution)/shard_map/ppermute | solution.py:360
  162.1 2.0 collective-permute-start.34
  162.6 4.1 %collective-permute-start.27 = (bf16[256,1024]{1,0:T(8,128)(2,1)S(1)}, bf16[256,1024]{1,0:T(8,128)(2,1)S(1)}, u32[]{:S(2)}, u32[]{:S(2)}) collective-permute-start(bf16[256,1024]{1,0:T(8,128)(2,1)S(1)} %fusion.1), channel_id=1, source_target_pairs={{0,4},{4,0},{1,5},{5,1},{2,6},{6,2},{3,7},{7,3},{8,12},{12,8},{9,1... | collective-permute-start | bytes 1572872 | tf_op jit(solution)/shard_map/ppermute | solution.py:360
  163.7 15.8 %collective-permute-start.38 = (bf16[128,1024]{1,0:T(8,128)(2,1)S(1)}, bf16[128,1024]{1,0:T(8,128)(2,1)S(1)}, u32[]{:S(2)}, u32[]{:S(2)}) collective-permute-start(bf16[128,1024]{1,0:T(8,128)(2,1)S(1)} %slice.162), channel_id=1, source_target_pairs={{0,2},{1,3},{2,0},{3,1},{4,6},{5,7},{6,4},{7,5},{8,10},{9,11},{10,... | collective-permute-start | bytes 786440 | tf_op jit(solution)/shard_map/ppermute | solution.py:360
  164.5 9.2 %collective-permute-start.35 = (bf16[128,1024]{1,0:T(8,128)(2,1)S(1)}, bf16[128,1024]{1,0:T(8,128)(2,1)S(1)}, u32[]{:S(2)}, u32[]{:S(2)}) collective-permute-start(bf16[128,1024]{1,0:T(8,128)(2,1)S(1)} %get-tuple-element.66), channel_id=1, source_target_pairs={{0,1},{1,0},{2,3},{3,2},{4,5},{5,4},{6,7},{7,6},{8,9},{9,8},{10,11... | collective-permute-start | bytes 786440 | tf_op jit(solution)/shard_map/ppermute | solution.py:360
  166.1 12.4 %collective-permute-start.39 = (bf16[128,1024]{1,0:T(8,128)(2,1)S(1)}, bf16[128,1024]{1,0:T(8,128)(2,1)S(1)}, u32[]{:S(2)}, u32[]{:S(2)}) collective-permute-start(bf16[128,1024]{1,0:T(8,128)(2,1)S(1)} %get-tuple-element.65), channel_id=1, source_target_pairs={{0,2},{1,3},{2,0},{3,1},{4,6},{5,7},{6,4},{7,5},{8,10},{9,11},{10,... | collective-permute-start | bytes 786440 | tf_op jit(solution)/shard_map/ppermute | solution.py:360
  167.2 12.3 %collective-permute-start.28 = (bf16[128,1024]{1,0:T(8,128)(2,1)S(1)}, bf16[128,1024]{1,0:T(8,128)(2,1)S(1)}, u32[]{:S(2)}, u32[]{:S(2)}) collective-permute-start(bf16[128,1024]{1,0:T(8,128)(2,1)S(1)} %slice.163), channel_id=1, source_target_pairs={{0,1},{1,0},{2,3},{3,2},{4,5},{5,4},{6,7},{7,6},{8,9},{9,8},{10,11... | collective-permute-start | bytes 786440 | tf_op jit(solution)/shard_map/ppermute | solution.py:360
  173.9 9.3 %collective-permute-start.36 = (bf16[128,1024]{1,0:T(8,128)(2,1)S(1)}, bf16[128,1024]{1,0:T(8,128)(2,1)S(1)}, u32[]{:S(2)}, u32[]{:S(2)}) collective-permute-start(bf16[128,1024]{1,0:T(8,128)(2,1)S(1)} %fusion.51), channel_id=1, source_target_pairs={{0,2},{1,3},{2,0},{3,1},{4,6},{5,7},{6,4},{7,5},{8,10},{9,11},{10,... | collective-permute-start | bytes 786440 | tf_op jit(solution)/shard_map/ppermute | solution.py:360
  178.6 6.5 %collective-permute-start.40 = (bf16[128,1024]{1,0:T(8,128)(2,1)S(1)}, bf16[128,1024]{1,0:T(8,128)(2,1)S(1)}, u32[]{:S(2)}, u32[]{:S(2)}) collective-permute-start(bf16[128,1024]{1,0:T(8,128)(2,1)S(1)} %fusion.48), channel_id=1, source_target_pairs={{0,1},{1,0},{2,3},{3,2},{4,5},{5,4},{6,7},{7,6},{8,9},{9,8},{10,11... | collective-permute-start | bytes 786440 | tf_op jit(solution)/shard_map/ppermute | solution.py:360
  185.4 11.2 %collective-permute-start.41 = (bf16[64,1024]{1,0:T(8,128)(2,1)S(1)}, bf16[64,1024]{1,0:T(8,128)(2,1)S(1)}, u32[]{:S(2)}, u32[]{:S(2)}) collective-permute-start(bf16[64,1024]{1,0:T(8,128)(2,1)S(1)} %get-tuple-element.70), channel_id=1, source_target_pairs={{0,16},{8,24},{16,0},{24,8},{1,17},{9,25},{17,1},{25,9},{2,18},{10... | collective-permute-start | bytes 393224 | tf_op jit(solution)/shard_map/ppermute | solution.py:347
  187.6 8.9 %collective-permute-start.42 = (bf16[64,1024]{1,0:T(8,128)(2,1)S(1)}, bf16[64,1024]{1,0:T(8,128)(2,1)S(1)}, u32[]{:S(2)}, u32[]{:S(2)}) collective-permute-start(bf16[64,1024]{1,0:T(8,128)(2,1)S(1)} %get-tuple-element.71), channel_id=1, source_target_pairs={{0,8},{8,16},{16,24},{24,0},{1,9},{9,17},{17,25},{25,1},{2,10},{10... | collective-permute-start | bytes 393224 | tf_op jit(solution)/shard_map/ppermute | solution.py:347
  190.4 6.8 %collective-permute-start.37 = (bf16[64,1024]{1,0:T(8,128)(2,1)S(1)}, bf16[64,1024]{1,0:T(8,128)(2,1)S(1)}, u32[]{:S(2)}, u32[]{:S(2)}) collective-permute-start(bf16[64,1024]{1,0:T(8,128)(2,1)S(1)} %slice.164), channel_id=1, source_target_pairs={{0,24},{8,0},{16,8},{24,16},{1,25},{9,1},{17,9},{25,17},{2,26},{10... | collective-permute-start | bytes 393224 | tf_op jit(solution)/shard_map/ppermute | solution.py:347
where the time goes:
time: 198 us
  waiting for transfers between devices  66.5 us (34%)
  starting transfers between devices  52.4 us (26%)
  Pallas kernels  44.5 us (22%)
  local copies, waits for them, and re-layouts  17.2 us (9%)
  matrix products  8.56 us (4%)
  other arithmetic  8.32 us (4%)
    pallas_call x1, Pallas kernels, attend(): pl.pallas_call(functools.partial(attend_kernel, pieces, base, listed, sub...  39.4 us
    ppermute x22, starting transfers between devices, shift(): lax.ppermute(value, axis, [(i, (i + step) % size) for i in range(size)])  37 us
    ppermute x21, waiting for transfers between devices, swap(): return lax.ppermute(value, axis, [(i, i ^ bits) for i in range(size)])  35.3 us
    ppermute x22, waiting for transfers between devices, shift(): lax.ppermute(value, axis, [(i, (i + step) % size) for i in range(size)])  31.2 us
    ppermute x21, starting transfers between devices, swap(): return lax.ppermute(value, axis, [(i, i ^ bits) for i in range(size)])  15.4 us
    unnamed x23, local copies, waits for them, and re-layouts  6.01 us
    pallas_call x1, Pallas kernels, merge_project(): pl.pallas_call(functools.partial(merge_kernel, parts, len(batches), share...  5.07 us
  transfers between devices with their start and end apart: 43, of which 19 were waited for; matrix products, arithmetic and copies ran while one was open for 14% of the time, Pallas kernels for 20%

commit v1 on v0

--- a/solution.py
+++ b/solution.py
@@ -380,7 +380,9 @@
         picked = lax.dynamic_index_in_dim(
             column, req_at * exp_size + (exp_at ^ bits), 1, keepdims=False
         )
-        return picked if bits == 0 else swap(picked, "exp", bits)
+        if bits == 0:
+            return picked
+        return swap(picked, "exp", bits)
 
     return [of(bits).reshape(-1) for bits in range(exp_size)]
 
@@ -411,11 +413,11 @@
     return kept, passed.astype(jnp.bfloat16)
 
 
-def dense_experts(half_hidden, row_weights, gains, maps_in, maps_out):
+def dense_experts(half_hidden, column_table, gains, maps_in, maps_out):
     row_count, half_width = half_hidden.shape
     req_size = lax.axis_size("req")
     sent = half_hidden.astype(jnp.bfloat16)
-    sent, row_weights = lax.optimization_barrier((sent, row_weights))
+    sent, column_table = lax.optimization_barrier((sent, column_table))
     column = jnp.concatenate(gather_blocks(sent, "req"), axis=0)
     middle = column.shape[0] // 2
 
@@ -430,6 +432,7 @@
 
     near_x = swap(column, "exp", 1)
     near_y = swap(column, "exp", 2)
+    row_weights = exchange_table(column_table)
     own_kept, own_passed = run(column, 0)
     near_x, near_y, own_passed = lax.optimization_barrier((near_x, near_y, own_passed))
     far_top = swap(near_x[:middle], "exp", 2)
@@ -544,9 +547,8 @@
         shift(take_block(split_weight, targets[s]), "exp", s) for s in range(1, exp_size)
     ]
     if dense:
-        column_table = jnp.stack(gather_blocks(route_table(route_ids, route_weights), "req"))
-        own_piece, column_table, flat_in = lax.optimization_barrier(
-            (pieces[0][0], column_table, expert_in[0].reshape(model_width, -1))
+        own_piece, flat_in = lax.optimization_barrier(
+            (pieces[0][0], expert_in[0].reshape(model_width, -1))
         )
         pieces[0] = [own_piece] + pieces[0][1:]
     received = []
@@ -570,8 +572,8 @@
     info = jnp.concatenate([jnp.stack([group_shift, head_at]).astype(jnp.int32), sources])
     kept, sent = merge_project(received, weight_parts, info, share, requests)
     if dense:
-        kept, column_table = lax.optimization_barrier((kept, column_table))
-        row_weights = exchange_table(column_table)
+        kept, named, given = lax.optimization_barrier((kept, route_ids, route_weights))
+        column_table = jnp.stack(gather_blocks(route_table(named, given), "req"))
     both = kept + shift(sent, "head", 1).astype(jnp.float32)
     both = both.reshape(exp_size, row_count, half_width)
     outgoing = both.astype(jnp.bfloat16)
@@ -582,7 +584,7 @@
         hidden = hidden + shift(take_block(outgoing, targets[s]), "exp", s).astype(jnp.float32)
 
     if dense:
-        mixture = dense_experts(hidden, row_weights, gains, maps_in, maps_out)
+        mixture = dense_experts(hidden, column_table, gains, maps_in, maps_out)
     else:
         mixture = sparse_experts(
             hidden, route_ids, route_weights, norm_gain, expert_in, expert_out, capacity

time: 198 us -> 183 us (0.924)
  waiting for transfers between devices: 66.5 us -> 51.7 us
  local copies, waits for them, and re-layouts: 17.2 us -> 14.1 us
  matrix products: 8.56 us -> 11.2 us
    ppermute x21, waiting for transfers between devices: 35.3 us -> 27.1 us  [swap(): return lax.ppermute(value, axis, [(i, i ^ bits) for i in range(size)])]
    ppermute x22, waiting for transfers between devices: 31.2 us -> 24.6 us  [shift(): lax.ppermute(value, axis, [(i, (i + step) % size) for i in range(size)])]
    reshape x4 -> x0, local copies, waits for them, and re-layouts: 2.36 us -> none  [exchange_table(): return [of(bits).reshape(-1) for bits in range(exp_size)]]
    reduce_sum x7, other arithmetic: 1.37 us -> 3.49 us  [expert_block(): squares = sum((jnp.sum(x * x, axis=-1, keepdims=True) for x in wide))]
  transfers between devices with their start and end apart: 43 -> 43, of which waited for: 19 -> 22; matrix products, arithmetic and copies ran while one was open for 14% -> 16% of each run, Pallas kernels for 20% -> 22%
where the time goes in v1:
time: 183 us; the launch traced here: 182 us
  starting transfers between devices  52.3 us (29%)
  waiting for transfers between devices  51.7 us (28%)
  Pallas kernels  44.5 us (24%)
  local copies, waits for them, and re-layouts  14.1 us (8%)
  matrix products  11.2 us (6%)
  other arithmetic  8.03 us (4%)
    pallas_call x1, Pallas kernels, attend(): pl.pallas_call(functools.partial(attend_kernel, pieces, base, listed, sub...  39.4 us
    ppermute x22, starting transfers between devices, shift(): lax.ppermute(value, axis, [(i, (i + step) % size) for i in range(size)])  37.1 us
    ppermute x21, waiting for transfers between devices, swap(): return lax.ppermute(value, axis, [(i, i ^ bits) for i in range(size)])  27.1 us
    ppermute x22, waiting for transfers between devices, shift(): lax.ppermute(value, axis, [(i, (i + step) % size) for i in range(size)])  24.6 us
    ppermute x21, starting transfers between devices, swap(): return lax.ppermute(value, axis, [(i, i ^ bits) for i in range(size)])  15.2 us
    pallas_call x1, Pallas kernels, merge_project(): pl.pallas_call(functools.partial(merge_kernel, parts, len(batches), share...  5.07 us
    unnamed x23, local copies, waits for them, and re-layouts  5.05 us
    dynamic_slice x2, local copies, waits for them, and re-layouts, halves(): other = lax.dynamic_slice_in_dim(value, (1 - head_at) * width, width, axis)  4.72 us
  transfers between devices with their start and end apart: 43, of which 22 were waited for; matrix products, arithmetic and copies ran while one was open for 16% of the time, Pallas kernels for 22%

profile of v1, /device:TPU:0, one launch (start us, length us, event | category | flops | bytes accessed | tf_op | source)
XLA Modules:
  0.0 182.3 jit_solution(6909908147764020224)
XLA Ops:
  0.0 3.0 %collective-permute-start = (bf16[4,16,16,128]{3,2,1,0:T(8,128)(2,1)}, bf16[4,16,16,128]{3,2,1,0:T(8,128)(2,1)S(1)}, u32[]{:S(2)}, u32[]{:S(2)}) collective-permute-start(bf16[4,16,16,128]{3,2,1,0:T(8,128)(2,1)} %refs_0_), channel_id=1, source_target_pairs={{0,1},{1,2},{2,3},{3,0},{4,5},{5,6},{6,7},{7,4},{8,9},{9,10},{10,1... | collective-permute-start | bytes 786440 | tf_op jit(solution)/shard_map/ppermute | solution.py:347
  3.0 1.5 collective-permute-start.1
  4.5 1.4 collective-permute-start.2
  5.9 3.1 %dynamic-slice_bitcast_fusion.2 = (bf16[512,512]{1,0:T(8,128)(2,1)}, bf16[512,512]{1,0:T(8,128)(2,1)}, bf16[512,512]{1,0:T(8,128)(2,1)}, bf16[512,512]{1,0:T(8,128)(2,1)}) fusion(bf16[4,512,512]{2,1,0:T(8,128)(2,1)} %bitcast.75, s32[]{:T(128)S(6)} %select_n.92, s32[]{:T(128)S(6)} %select_n.90, s32[]{:T(128)S(6)} %select_n.88, s32[]{:T(128)S(6)} %select_n.86), kind=kLoop, calls=%fused_computation.97 | loop fusion | bytes 4194320 | tf_op jit(solution)/shard_map/jit(dynamic_index_in_dim)/squeeze | solution.py:351
  10.1 2.3 %copy.16 = bf16[256,8,2,384]{3,1,2,0:T(8,128)(2,1)} copy(bf16[256,8,2,384]{3,2,1,0:T(2,128)(2,1)S(1)} %bitcast.74) | data formatting | bytes 6291456
  12.4 1.9 %collective-permute-start.8 = (bf16[512,512]{1,0:T(8,128)(2,1)}, bf16[512,512]{1,0:T(8,128)(2,1)}, u32[]{:S(2)}, u32[]{:S(2)}) collective-permute-start(bf16[512,512]{1,0:T(8,128)(2,1)} %get-tuple-element.51), channel_id=1, source_target_pairs={{0,3},{1,0},{2,1},{3,2},{4,7},{5,4},{6,5},{7,6},{8,11},{9,8},{10,9... | collective-permute-start | bytes 1572872 | tf_op jit(solution)/shard_map/ppermute | solution.py:347
  14.9 1.5 dynamic-slice_bitcast_fusion
  16.4 0.7 collective-permute-done.1.refs_2_
  17.6 39.4 %attend.1 = (bf16[64,2176]{1,0:T(8,128)(2,1)}, bf16[64,2176]{1,0:T(8,128)(2,1)}, bf16[64,2176]{1,0:T(8,128)(2,1)}, bf16[64,2176]{1,0:T(8,128)(2,1)}) custom-call(s32[8]{0:T(128)} %pad_add_fusion.1.info_ref, bf16[4,16,16,128]{3,2,1,0:T(8,128)(2,1)} %refs_0_, bf16[4,16,16,128]{3,2,1,0:T(8,128)(2,1)} %copy-done.3, ...), custom_call_target="tpu_custom_call" | custom-call | tf_op jit(solution)/shard_map/attend/pallas_call | solution.py:243
  57.1 2.8 %collective-permute-start.5 = (bf16[64,2176]{1,0:T(8,128)(2,1)}, bf16[64,2176]{1,0:T(8,128)(2,1)}, u32[]{:S(2)}, u32[]{:S(2)}) collective-permute-start(bf16[64,2176]{1,0:T(8,128)(2,1)} %get-tuple-element.32), channel_id=1, source_target_pairs={{0,3},{1,0},{2,1},{3,2},{4,7},{5,4},{6,5},{7,6},{8,11},{9,8},{10,9... | collective-permute-start | bytes 835592 | tf_op jit(solution)/shard_map/ppermute | solution.py:347
  60.5 3.2 %constant_dynamic-slice_fusion.4 = (bf16[1024,768]{1,0:T(8,128)(2,1)}, bf16[1024,768]{1,0:T(8,128)(2,1)S(1)}) fusion(bf16[2048,768]{1,0:T(8,128)(2,1)} %bitcast.71, s32[]{:T(128)S(6)} %select_n.84, s32[]{:T(128)S(6)} %select_n.80), kind=kLoop, calls=%fused_computation.135 | loop fusion | bytes 6291464 | tf_op jit(solution)/shard_map/dynamic_slice | solution.py:393
  63.8 3.9 %collective-permute-done.3.refs_1_ = bf16[64,2176]{1,0:T(8,128)(2,1)S(1)} collective-permute-done((bf16[64,2176]{1,0:T(8,128)(2,1)}, bf16[64,2176]{1,0:T(8,128)(2,1)S(1)}, u32[]{:S(2)}, u32[]{:S(2)}) %collective-permute-start.3) | collective-permute-done | bytes 278560 | tf_op jit(solution)/shard_map/ppermute | solution.py:347
  67.6 3.6 %collective-permute-done.4.refs_2_ = bf16[64,2176]{1,0:T(8,128)(2,1)} collective-permute-done((bf16[64,2176]{1,0:T(8,128)(2,1)}, bf16[64,2176]{1,0:T(8,128)(2,1)}, u32[]{:S(2)}, u32[]{:S(2)}) %collective-permute-start.4) | collective-permute-done | bytes 278560 | tf_op jit(solution)/shard_map/ppermute | solution.py:347
  71.2 5.1 %merge_project.1 = (f32[256,1024]{1,0:T(8,128)}, bf16[256,1024]{1,0:T(8,128)(2,1)}) custom-call(s32[6]{0:T(128)} %pad_add_fusion.info_ref, bf16[64,2176]{1,0:T(8,128)(2,1)} %get-tuple-element.29.refs_0_, bf16[64,2176]{1,0:T(8,128)(2,1)} %copy-done.2, bf16[64,2176]{1,0:T(8,128)(2,1)} %collective-permute-done.4.refs_2_, ...), custom_call_target="tpu_custom_call" | custom-call | tf_op jit(solution)/shard_map/merge_project/pallas_call | solution.py:327
  76.3 2.1 %collective-permute-done.9 = bf16[256,1024]{1,0:T(8,128)(2,1)S(1)} collective-permute-done((bf16[256,1024]{1,0:T(8,128)(2,1)}, bf16[256,1024]{1,0:T(8,128)(2,1)S(1)}, u32[]{:S(2)}, u32[]{:S(2)}) %collective-permute-start.9) | collective-permute-done | bytes 524320 | tf_op jit(solution)/shard_map/ppermute | solution.py:347
  78.4 1.4 convert_add_fusion.1
  80.0 1.4 collective-permute-start.10
  81.4 1.8 collective-permute-start.11
  83.2 1.2 collective-permute-start.12
  84.4 8.1 %collective-permute-start.13 = (f32[16,64]{1,0:T(8,128)S(1)}, f32[16,64]{1,0:T(8,128)S(1)}, u32[]{:S(2)}, u32[]{:S(2)}) collective-permute-start(f32[16,64]{1,0:T(8,128)S(1)} %select_reduce_fusion), channel_id=1, source_target_pairs={{0,8},{8,16},{16,24},{24,0},{1,9},{9,17},{17,25},{25,1},{2,10},{10... | collective-permute-start | bytes 12296 | tf_op jit(solution)/shard_map/ppermute | solution.py:347
  92.5 0.7 collective-permute-start.14
  93.2 1.1 collective-permute-done.13
  94.3 2.0 %collective-permute-start.15 = (f32[16,64]{1,0:T(8,128)S(1)}, f32[16,64]{1,0:T(8,128)S(1)}, u32[]{:S(2)}, u32[]{:S(2)}) collective-permute-start(f32[16,64]{1,0:T(8,128)S(1)} %select_reduce_fusion), channel_id=1, source_target_pairs={{0,24},{8,0},{16,8},{24,16},{1,25},{9,1},{17,9},{25,17},{2,26},{10... | collective-permute-start | bytes 12296 | tf_op jit(solution)/shard_map/ppermute | solution.py:347
  96.3 0.8 collective-permute-done.14
  97.0 0.9 collective-permute-done.15
  98.1 1.9 %collective-permute-start.16 = (bf16[64,1024]{1,0:T(8,128)(2,1)S(1)}, bf16[64,1024]{1,0:T(8,128)(2,1)S(1)}, u32[]{:S(2)}, u32[]{:S(2)}) collective-permute-start(bf16[64,1024]{1,0:T(8,128)(2,1)S(1)} %get-tuple-element.38), channel_id=1, source_target_pairs={{0,8},{8,16},{16,24},{24,0},{1,9},{9,17},{17,25},{25,1},{2,10},{10... | collective-permute-start | bytes 393224 | tf_op jit(solution)/shard_map/ppermute | solution.py:347
  100.0 2.6 %collective-permute-start.17 = (bf16[64,1024]{1,0:T(8,128)(2,1)S(1)}, bf16[64,1024]{1,0:T(8,128)(2,1)S(1)}, u32[]{:S(2)}, u32[]{:S(2)}) collective-permute-start(bf16[64,1024]{1,0:T(8,128)(2,1)S(1)} %get-tuple-element.38), channel_id=1, source_target_pairs={{0,16},{8,24},{16,0},{24,8},{1,17},{9,25},{17,1},{25,9},{2,18},{10... | collective-permute-start | bytes 393224 | tf_op jit(solution)/shard_map/ppermute | solution.py:347
  102.6 0.6 constant_dynamic-update-slice_fusion.3
  103.2 2.5 %collective-permute-done.16 = bf16[64,1024]{1,0:T(8,128)(2,1)S(1)} collective-permute-done((bf16[64,1024]{1,0:T(8,128)(2,1)S(1)}, bf16[64,1024]{1,0:T(8,128)(2,1)S(1)}, u32[]{:S(2)}, u32[]{:S(2)}) %collective-permute-start.16) | collective-permute-done | bytes 131104 | tf_op jit(solution)/shard_map/ppermute | solution.py:347
  105.8 0.7 constant_dynamic-update-slice_fusion.2
  106.4 3.2 %collective-permute-done.17 = bf16[64,1024]{1,0:T(8,128)(2,1)S(1)} collective-permute-done((bf16[64,1024]{1,0:T(8,128)(2,1)S(1)}, bf16[64,1024]{1,0:T(8,128)(2,1)S(1)}, u32[]{:S(2)}, u32[]{:S(2)}) %collective-permute-start.17) | collective-permute-done | bytes 131104 | tf_op jit(solution)/shard_map/ppermute | solution.py:347
  109.6 0.7 constant_dynamic-update-slice_fusion.1
  110.3 0.7 constant_dynamic-update-slice_fusion
  111.0 0.6 collective-permute-start.28
  111.6 1.7 collective-permute-start.33
  113.3 1.2 collective-permute-start.24
  114.7 1.4 collective-permute-done.33
  116.2 0.7 collective-permute-done.24
  117.0 1.2 collective-permute-start.20
  118.8 1.3 fusion.8
  120.0 1.2 fusion.11
  121.3 2.2 %fusion.45 = f32[256,768]{1,0:T(8,128)S(1)} fusion(bf16[1024,768]{1,0:T(8,128)(2,1)} %get-tuple-element.40, bf16[256,1024]{1,0:T(8,128)(2,1)} %collective-permute-done.19, f32[1024]{0:T(1024)S(1)} %get-tuple-element.71, f32[256]{0:T(256)S(1)} %add_rsqrt_fusion.3), kind=kOutput, calls=%fused_computation.67 | convolution fusion | flops 403701760 | bytes 2888704 | tf_op jit(solution)/shard_map/dot_general | solution.py:404
  123.5 1.7 fusion.49
  125.7 4.4 %collective-permute-done.20 = bf16[256,1024]{1,0:T(8,128)(2,1)S(1)} collective-permute-done((bf16[256,1024]{1,0:T(8,128)(2,1)}, bf16[256,1024]{1,0:T(8,128)(2,1)S(1)}, u32[]{:S(2)}, u32[]{:S(2)}) %collective-permute-start.20) | collective-permute-done | bytes 524320 | tf_op jit(solution)/shard_map/ppermute | solution.py:360
  130.1 0.6 collective-permute-done.21
  132.0 1.2 collective-permute-start.31
  133.9 5.7 %collective-permute-done.30 = bf16[128,1024]{1,0:T(8,128)(2,1)S(1)} collective-permute-done((bf16[128,1024]{1,0:T(8,128)(2,1)S(1)}, bf16[128,1024]{1,0:T(8,128)(2,1)S(1)}, u32[]{:S(2)}, u32[]{:S(2)}) %collective-permute-start.30) | collective-permute-done | bytes 262176 | tf_op jit(solution)/shard_map/ppermute | solution.py:360
  141.1 0.8 copy-done
  145.5 0.6 fusion.32
  148.9 1.5 collective-permute-start.38
  150.9 1.2 collective-permute-start.35
  152.0 0.7 collective-permute-start.39
  153.2 0.9 collective-permute-start.26
  154.1 6.0 %collective-permute-done.35 = bf16[128,1024]{1,0:T(8,128)(2,1)S(1)} collective-permute-done((bf16[128,1024]{1,0:T(8,128)(2,1)S(1)}, bf16[128,1024]{1,0:T(8,128)(2,1)S(1)}, u32[]{:S(2)}, u32[]{:S(2)}) %collective-permute-start.35) | collective-permute-done | bytes 262176 | tf_op jit(solution)/shard_map/ppermute | solution.py:360
  160.2 0.7 collective-permute-start.36
  160.9 2.9 %collective-permute-done.39 = bf16[128,1024]{1,0:T(8,128)(2,1)S(1)} collective-permute-done((bf16[128,1024]{1,0:T(8,128)(2,1)S(1)}, bf16[128,1024]{1,0:T(8,128)(2,1)S(1)}, u32[]{:S(2)}, u32[]{:S(2)}) %collective-permute-start.39) | collective-permute-done | bytes 262176 | tf_op jit(solution)/shard_map/ppermute | solution.py:360
  163.8 1.3 collective-permute-start.40
  165.3 3.1 %collective-permute-done.36 = bf16[128,1024]{1,0:T(8,128)(2,1)S(1)} collective-permute-done((bf16[128,1024]{1,0:T(8,128)(2,1)S(1)}, bf16[128,1024]{1,0:T(8,128)(2,1)S(1)}, u32[]{:S(2)}, u32[]{:S(2)}) %collective-permute-start.36) | collective-permute-done | bytes 262176 | tf_op jit(solution)/shard_map/ppermute | solution.py:360
  168.4 1.9 %collective-permute-done.40 = bf16[128,1024]{1,0:T(8,128)(2,1)S(1)} collective-permute-done((bf16[128,1024]{1,0:T(8,128)(2,1)S(1)}, bf16[128,1024]{1,0:T(8,128)(2,1)S(1)}, u32[]{:S(2)}, u32[]{:S(2)}) %collective-permute-start.40) | collective-permute-done | bytes 262176 | tf_op jit(solution)/shard_map/ppermute | solution.py:360
  170.6 1.6 collective-permute-start.41
  172.2 2.2 %collective-permute-start.42 = (bf16[64,1024]{1,0:T(8,128)(2,1)S(1)}, bf16[64,1024]{1,0:T(8,128)(2,1)S(1)}, u32[]{:S(2)}, u32[]{:S(2)}) collective-permute-start(bf16[64,1024]{1,0:T(8,128)(2,1)S(1)} %get-tuple-element.65), channel_id=1, source_target_pairs={{0,8},{8,16},{16,24},{24,0},{1,9},{9,17},{17,25},{25,1},{2,10},{10... | collective-permute-start | bytes 393224 | tf_op jit(solution)/shard_map/ppermute | solution.py:347
  174.4 1.7 collective-permute-start.37
  176.1 5.1 %collective-permute-done.41 = bf16[64,1024]{1,0:T(8,128)(2,1)S(1)} collective-permute-done((bf16[64,1024]{1,0:T(8,128)(2,1)S(1)}, bf16[64,1024]{1,0:T(8,128)(2,1)S(1)}, u32[]{:S(2)}, u32[]{:S(2)}) %collective-permute-start.41) | collective-permute-done | bytes 131104 | tf_op jit(solution)/shard_map/ppermute | solution.py:347
  181.5 0.7 fusion.80
  (111 shorter events, 16.2 us)
Async XLA Ops:
  0.0 12.4 %collective-permute-start = (bf16[4,16,16,128]{3,2,1,0:T(8,128)(2,1)}, bf16[4,16,16,128]{3,2,1,0:T(8,128)(2,1)S(1)}, u32[]{:S(2)}, u32[]{:S(2)}) collective-permute-start(bf16[4,16,16,128]{3,2,1,0:T(8,128)(2,1)} %refs_0_), channel_id=1, source_target_pairs={{0,1},{1,2},{2,3},{3,0},{4,5},{5,6},{6,7},{7,4},{8,9},{9,10},{10,1... | collective-permute-start | bytes 786440 | tf_op jit(solution)/shard_map/ppermute | solution.py:347
  3.0 14.1 %collective-permute-start.1 = (bf16[4,16,16,128]{3,2,1,0:T(8,128)(2,1)}, bf16[4,16,16,128]{3,2,1,0:T(8,128)(2,1)}, u32[]{:S(2)}, u32[]{:S(2)}) collective-permute-start(bf16[4,16,16,128]{3,2,1,0:T(8,128)(2,1)} %refs_0_), channel_id=1, source_target_pairs={{0,2},{1,3},{2,0},{3,1},{4,6},{5,7},{6,4},{7,5},{8,10},{9,11},{10,... | collective-permute-start | bytes 786440 | tf_op jit(solution)/shard_map/ppermute | solution.py:347
  4.5 13.1 %collective-permute-start.2 = (bf16[4,16,16,128]{3,2,1,0:T(8,128)(2,1)}, bf16[4,16,16,128]{3,2,1,0:T(8,128)(2,1)}, u32[]{:S(2)}, u32[]{:S(2)}) collective-permute-start(bf16[4,16,16,128]{3,2,1,0:T(8,128)(2,1)} %refs_0_), channel_id=1, source_target_pairs={{0,3},{1,0},{2,1},{3,2},{4,7},{5,4},{6,5},{7,6},{8,11},{9,8},{10,9... | collective-permute-start | bytes 786440 | tf_op jit(solution)/shard_map/ppermute | solution.py:347
  5.9 4.2 %copy-start.1 = (bf16[1,2048,2,384]{3,2,1,0:T(2,128)(2,1)S(1)}, bf16[1,2048,2,384]{3,2,1,0:T(2,128)(2,1)}, u32[]{:S(2)}) copy-start(bf16[1,2048,2,384]{3,2,1,0:T(2,128)(2,1)} %param.24) | copy-start | bytes 9437188
  9.0 48.1 %collective-permute-start.6 = (bf16[512,512]{1,0:T(8,128)(2,1)}, bf16[512,512]{1,0:T(8,128)(2,1)}, u32[]{:S(2)}, u32[]{:S(2)}) collective-permute-start(bf16[512,512]{1,0:T(8,128)(2,1)} %get-tuple-element.53), channel_id=1, source_target_pairs={{0,1},{1,2},{2,3},{3,0},{4,5},{5,6},{6,7},{7,4},{8,9},{9,10},{10,1... | collective-permute-start | bytes 1572872 | tf_op jit(solution)/shard_map/ppermute | solution.py:347
  9.6 54.2 %collective-permute-start.7 = (bf16[512,512]{1,0:T(8,128)(2,1)}, bf16[512,512]{1,0:T(8,128)(2,1)}, u32[]{:S(2)}, u32[]{:S(2)}) collective-permute-start(bf16[512,512]{1,0:T(8,128)(2,1)} %get-tuple-element.52), channel_id=1, source_target_pairs={{0,2},{1,3},{2,0},{3,1},{4,6},{5,7},{6,4},{7,5},{8,10},{9,11},{10,... | collective-permute-start | bytes 1572872 | tf_op jit(solution)/shard_map/ppermute | solution.py:347
  10.1 2.3 %copy-start.8 = (s32[4]{0:T(128)S(1)}, s32[4]{0:T(128)}, u32[]{:S(2)}) copy-start(s32[4]{0:T(128)} %param.18) | copy-start | bytes 52
  12.4 4.0 %copy-start.3 = (bf16[4,16,16,128]{3,2,1,0:T(8,128)(2,1)}, bf16[4,16,16,128]{3,2,1,0:T(8,128)(2,1)S(1)}, u32[]{:S(2)}) copy-start(bf16[4,16,16,128]{3,2,1,0:T(8,128)(2,1)S(1)} %collective-permute-done.refs_1_) | copy-start | bytes 786436
  12.4 51.4 %collective-permute-start.8 = (bf16[512,512]{1,0:T(8,128)(2,1)}, bf16[512,512]{1,0:T(8,128)(2,1)}, u32[]{:S(2)}, u32[]{:S(2)}) collective-permute-start(bf16[512,512]{1,0:T(8,128)(2,1)} %get-tuple-element.51), channel_id=1, source_target_pairs={{0,3},{1,0},{2,1},{3,2},{4,7},{5,4},{6,5},{7,6},{8,11},{9,8},{10,9... | collective-permute-start | bytes 1572872 | tf_op jit(solution)/shard_map/ppermute | solution.py:347
  57.0 10.6 %collective-permute-start.3 = (bf16[64,2176]{1,0:T(8,128)(2,1)}, bf16[64,2176]{1,0:T(8,128)(2,1)S(1)}, u32[]{:S(2)}, u32[]{:S(2)}) collective-permute-start(bf16[64,2176]{1,0:T(8,128)(2,1)} %get-tuple-element.30), channel_id=1, source_target_pairs={{0,1},{1,2},{2,3},{3,0},{4,5},{5,6},{6,7},{7,4},{8,9},{9,10},{10,1... | collective-permute-start | bytes 835592 | tf_op jit(solution)/shard_map/ppermute | solution.py:347
  57.0 14.2 %collective-permute-start.4 = (bf16[64,2176]{1,0:T(8,128)(2,1)}, bf16[64,2176]{1,0:T(8,128)(2,1)}, u32[]{:S(2)}, u32[]{:S(2)}) collective-permute-start(bf16[64,2176]{1,0:T(8,128)(2,1)} %get-tuple-element.31), channel_id=1, source_target_pairs={{0,2},{1,3},{2,0},{3,1},{4,6},{5,7},{6,4},{7,5},{8,10},{9,11},{10,... | collective-permute-start | bytes 835592 | tf_op jit(solution)/shard_map/ppermute | solution.py:347
  57.1 14.1 %collective-permute-start.5 = (bf16[64,2176]{1,0:T(8,128)(2,1)}, bf16[64,2176]{1,0:T(8,128)(2,1)}, u32[]{:S(2)}, u32[]{:S(2)}) collective-permute-start(bf16[64,2176]{1,0:T(8,128)(2,1)} %get-tuple-element.32), channel_id=1, source_target_pairs={{0,3},{1,0},{2,1},{3,2},{4,7},{5,4},{6,5},{7,6},{8,11},{9,8},{10,9... | collective-permute-start | bytes 835592 | tf_op jit(solution)/shard_map/ppermute | solution.py:347
  67.6 3.6 %copy-start.2 = (bf16[64,2176]{1,0:T(8,128)(2,1)}, bf16[64,2176]{1,0:T(8,128)(2,1)S(1)}, u32[]{:S(2)}) copy-start(bf16[64,2176]{1,0:T(8,128)(2,1)S(1)} %collective-permute-done.3.refs_1_) | copy-start | bytes 835588
  76.3 2.1 %collective-permute-start.9 = (bf16[256,1024]{1,0:T(8,128)(2,1)}, bf16[256,1024]{1,0:T(8,128)(2,1)S(1)}, u32[]{:S(2)}, u32[]{:S(2)}) collective-permute-start(bf16[256,1024]{1,0:T(8,128)(2,1)} %get-tuple-element.35), channel_id=1, source_target_pairs={{0,4},{4,0},{1,5},{5,1},{2,6},{6,2},{3,7},{7,3},{8,12},{12,8},{9,1... | collective-permute-start | bytes 1572872 | tf_op jit(solution)/shard_map/ppermute | solution.py:347
  79.8 4.6 %copy-start.6 = (f32[64,8]{0,1:T(8,128)S(1)}, f32[64,8]{0,1:T(8,128)}, u32[]{:S(2)}) copy-start(f32[64,8]{0,1:T(8,128)} %param.23) | copy-start | bytes 6148
  79.8 4.6 %copy-start.7 = (s32[64,8]{0,1:T(8,128)S(1)}, s32[64,8]{0,1:T(8,128)}, u32[]{:S(2)}) copy-start(s32[64,8]{0,1:T(8,128)} %param.22) | copy-start | bytes 6148
  79.8 18.1 %copy-start.4 = (bf16[64,2048]{1,0:T(8,128)(2,1)S(1)}, bf16[64,2048]{1,0:T(8,128)(2,1)}, u32[]{:S(2)}) copy-start(bf16[64,2048]{1,0:T(8,128)(2,1)} %param.19) | copy-start | bytes 786436
  79.9 34.6 %copy-start.5 = (f32[2048]{0:T(1024)S(1)}, f32[2048]{0:T(1024)}, u32[]{:S(2)}) copy-start(f32[2048]{0:T(1024)} %param.21) | copy-start | bytes 24580
  80.0 18.0 %collective-permute-start.10 = (bf16[64,1024]{1,0:T(8,128)(2,1)S(1)}, bf16[64,1024]{1,0:T(8,128)(2,1)S(1)}, u32[]{:S(2)}, u32[]{:S(2)}) collective-permute-start(bf16[64,1024]{1,0:T(8,128)(2,1)S(1)} %get-tuple-element.61), channel_id=1, source_target_pairs={{0,1},{1,2},{2,3},{3,0},{4,5},{5,6},{6,7},{7,4},{8,9},{9,10},{10,1... | collective-permute-start | bytes 393224 | tf_op jit(solution)/shard_map/ppermute | solution.py:347
  81.4 16.5 %collective-permute-start.11 = (bf16[64,1024]{1,0:T(8,128)(2,1)S(1)}, bf16[64,1024]{1,0:T(8,128)(2,1)S(1)}, u32[]{:S(2)}, u32[]{:S(2)}) collective-permute-start(bf16[64,1024]{1,0:T(8,128)(2,1)S(1)} %get-tuple-element.63), channel_id=1, source_target_pairs={{0,2},{1,3},{2,0},{3,1},{4,6},{5,7},{6,4},{7,5},{8,10},{9,11},{10,... | collective-permute-start | bytes 393224 | tf_op jit(solution)/shard_map/ppermute | solution.py:347
  83.2 14.8 %collective-permute-start.12 = (bf16[64,1024]{1,0:T(8,128)(2,1)S(1)}, bf16[64,1024]{1,0:T(8,128)(2,1)S(1)}, u32[]{:S(2)}, u32[]{:S(2)}) collective-permute-start(bf16[64,1024]{1,0:T(8,128)(2,1)S(1)} %get-tuple-element.62), channel_id=1, source_target_pairs={{0,3},{1,0},{2,1},{3,2},{4,7},{5,4},{6,5},{7,6},{8,11},{9,8},{10,9... | collective-permute-start | bytes 393224 | tf_op jit(solution)/shard_map/ppermute | solution.py:347
  84.4 9.8 %collective-permute-start.13 = (f32[16,64]{1,0:T(8,128)S(1)}, f32[16,64]{1,0:T(8,128)S(1)}, u32[]{:S(2)}, u32[]{:S(2)}) collective-permute-start(f32[16,64]{1,0:T(8,128)S(1)} %select_reduce_fusion), channel_id=1, source_target_pairs={{0,8},{8,16},{16,24},{24,0},{1,9},{9,17},{17,25},{25,1},{2,10},{10... | collective-permute-start | bytes 12296 | tf_op jit(solution)/shard_map/ppermute | solution.py:347
  92.5 4.5 %collective-permute-start.14 = (f32[16,64]{1,0:T(8,128)S(1)}, f32[16,64]{1,0:T(8,128)S(1)}, u32[]{:S(2)}, u32[]{:S(2)}) collective-permute-start(f32[16,64]{1,0:T(8,128)S(1)} %select_reduce_fusion), channel_id=1, source_target_pairs={{0,16},{8,24},{16,0},{24,8},{1,17},{9,25},{17,1},{25,9},{2,18},{10... | collective-permute-start | bytes 12296 | tf_op jit(solution)/shard_map/ppermute | solution.py:347
  94.3 3.7 %collective-permute-start.15 = (f32[16,64]{1,0:T(8,128)S(1)}, f32[16,64]{1,0:T(8,128)S(1)}, u32[]{:S(2)}, u32[]{:S(2)}) collective-permute-start(f32[16,64]{1,0:T(8,128)S(1)} %select_reduce_fusion), channel_id=1, source_target_pairs={{0,24},{8,0},{16,8},{24,16},{1,25},{9,1},{17,9},{25,17},{2,26},{10... | collective-permute-start | bytes 12296 | tf_op jit(solution)/shard_map/ppermute | solution.py:347
  98.1 7.7 %collective-permute-start.16 = (bf16[64,1024]{1,0:T(8,128)(2,1)S(1)}, bf16[64,1024]{1,0:T(8,128)(2,1)S(1)}, u32[]{:S(2)}, u32[]{:S(2)}) collective-permute-start(bf16[64,1024]{1,0:T(8,128)(2,1)S(1)} %get-tuple-element.38), channel_id=1, source_target_pairs={{0,8},{8,16},{16,24},{24,0},{1,9},{9,17},{17,25},{25,1},{2,10},{10... | collective-permute-start | bytes 393224 | tf_op jit(solution)/shard_map/ppermute | solution.py:347
  100.0 9.6 %collective-permute-start.17 = (bf16[64,1024]{1,0:T(8,128)(2,1)S(1)}, bf16[64,1024]{1,0:T(8,128)(2,1)S(1)}, u32[]{:S(2)}, u32[]{:S(2)}) collective-permute-start(bf16[64,1024]{1,0:T(8,128)(2,1)S(1)} %get-tuple-element.38), channel_id=1, source_target_pairs={{0,16},{8,24},{16,0},{24,8},{1,17},{9,25},{17,1},{25,9},{2,18},{10... | collective-permute-start | bytes 393224 | tf_op jit(solution)/shard_map/ppermute | solution.py:347
  103.2 7.0 %collective-permute-start.18 = (bf16[64,1024]{1,0:T(8,128)(2,1)S(1)}, bf16[64,1024]{1,0:T(8,128)(2,1)S(1)}, u32[]{:S(2)}, u32[]{:S(2)}) collective-permute-start(bf16[64,1024]{1,0:T(8,128)(2,1)S(1)} %get-tuple-element.38), channel_id=1, source_target_pairs={{0,24},{8,0},{16,8},{24,16},{1,25},{9,1},{17,9},{25,17},{2,26},{10... | collective-permute-start | bytes 393224 | tf_op jit(solution)/shard_map/ppermute | solution.py:347
  110.9 9.1 %collective-permute-start.19 = (bf16[256,1024]{1,0:T(8,128)(2,1)}, bf16[256,1024]{1,0:T(8,128)(2,1)}, u32[]{:S(2)}, u32[]{:S(2)}) collective-permute-start(bf16[256,1024]{1,0:T(8,128)(2,1)} %constant_dynamic-update-slice_fusion), channel_id=1, source_target_pairs={{0,4},{4,0},{1,5},{5,1},{2,6},{6,2},{3,7},{7,3},{8,12},{12,8},{9,1... | collective-permute-start | bytes 1572872 | tf_op jit(solution)/shard_map/ppermute | solution.py:360
  111.0 3.6 %collective-permute-start.28 = (f32[4,64]{1,0:T(4,128)S(1)}, f32[4,64]{1,0:T(4,128)S(1)}, u32[]{:S(2)}, u32[]{:S(2)}) collective-permute-start(f32[4,64]{1,0:T(4,128)S(1)} %bitcast.84), channel_id=1, source_target_pairs={{0,2},{1,3},{2,0},{3,1},{4,6},{5,7},{6,4},{7,5},{8,10},{9,11},{10,... | collective-permute-start | bytes 3080 | tf_op jit(solution)/shard_map/ppermute | solution.py:360
  111.6 4.5 %collective-permute-start.33 = (f32[4,64]{1,0:T(4,128)S(1)}, f32[4,64]{1,0:T(4,128)S(1)}, u32[]{:S(2)}, u32[]{:S(2)}) collective-permute-start(f32[4,64]{1,0:T(4,128)S(1)} %bitcast.83), channel_id=1, source_target_pairs={{0,3},{1,2},{2,1},{3,0},{4,7},{5,6},{6,5},{7,4},{8,11},{9,10},{10,... | collective-permute-start | bytes 3080 | tf_op jit(solution)/shard_map/ppermute | solution.py:360
  113.3 3.6 %collective-permute-start.24 = (f32[4,64]{1,0:T(4,128)S(1)}, f32[4,64]{1,0:T(4,128)S(1)}, u32[]{:S(2)}, u32[]{:S(2)}) collective-permute-start(f32[4,64]{1,0:T(4,128)S(1)} %bitcast.82), channel_id=1, source_target_pairs={{0,1},{1,0},{2,3},{3,2},{4,5},{5,4},{6,7},{7,6},{8,9},{9,8},{10,11... | collective-permute-start | bytes 3080 | tf_op jit(solution)/shard_map/ppermute | solution.py:360
  117.0 13.1 %collective-permute-start.20 = (bf16[256,1024]{1,0:T(8,128)(2,1)}, bf16[256,1024]{1,0:T(8,128)(2,1)S(1)}, u32[]{:S(2)}, u32[]{:S(2)}) collective-permute-start(bf16[256,1024]{1,0:T(8,128)(2,1)} %constant_dynamic-update-slice_fusion), channel_id=1, source_target_pairs={{0,1},{1,0},{2,3},{3,2},{4,5},{5,4},{6,7},{7,6},{8,9},{9,8},{10,11... | collective-permute-start | bytes 1572872 | tf_op jit(solution)/shard_map/ppermute | solution.py:360
  118.2 12.6 %collective-permute-start.21 = (bf16[256,1024]{1,0:T(8,128)(2,1)}, bf16[256,1024]{1,0:T(8,128)(2,1)S(1)}, u32[]{:S(2)}, u32[]{:S(2)}) collective-permute-start(bf16[256,1024]{1,0:T(8,128)(2,1)} %constant_dynamic-update-slice_fusion), channel_id=1, source_target_pairs={{0,2},{1,3},{2,0},{3,1},{4,6},{5,7},{6,4},{7,5},{8,10},{9,11},{10,... | collective-permute-start | bytes 1572872 | tf_op jit(solution)/shard_map/ppermute | solution.py:360
  130.8 9.5 %collective-permute-start.27 = (bf16[256,1024]{1,0:T(8,128)(2,1)S(1)}, bf16[256,1024]{1,0:T(8,128)(2,1)S(1)}, u32[]{:S(2)}, u32[]{:S(2)}) collective-permute-start(bf16[256,1024]{1,0:T(8,128)(2,1)S(1)} %collective-permute-done.21), channel_id=1, source_target_pairs={{0,4},{4,0},{1,5},{5,1},{2,6},{6,2},{3,7},{7,3},{8,12},{12,8},{9,1... | collective-permute-start | bytes 1572872 | tf_op jit(solution)/shard_map/ppermute | solution.py:360
  130.8 12.9 %collective-permute-start.23 = (bf16[256,1024]{1,0:T(8,128)(2,1)S(1)}, bf16[256,1024]{1,0:T(8,128)(2,1)S(1)}, u32[]{:S(2)}, u32[]{:S(2)}) collective-permute-start(bf16[256,1024]{1,0:T(8,128)(2,1)S(1)} %collective-permute-done.20), channel_id=1, source_target_pairs={{0,4},{4,0},{1,5},{5,1},{2,6},{6,2},{3,7},{7,3},{8,12},{12,8},{9,1... | collective-permute-start | bytes 1572872 | tf_op jit(solution)/shard_map/ppermute | solution.py:360
  131.4 8.3 %collective-permute-start.30 = (bf16[128,1024]{1,0:T(8,128)(2,1)S(1)}, bf16[128,1024]{1,0:T(8,128)(2,1)S(1)}, u32[]{:S(2)}, u32[]{:S(2)}) collective-permute-start(bf16[128,1024]{1,0:T(8,128)(2,1)S(1)} %slice.87), channel_id=1, source_target_pairs={{0,2},{1,3},{2,0},{3,1},{4,6},{5,7},{6,4},{7,5},{8,10},{9,11},{10,... | collective-permute-start | bytes 786440 | tf_op jit(solution)/shard_map/ppermute | solution.py:360
  132.0 8.0 %collective-permute-start.31 = (bf16[128,1024]{1,0:T(8,128)(2,1)S(1)}, bf16[128,1024]{1,0:T(8,128)(2,1)S(1)}, u32[]{:S(2)}, u32[]{:S(2)}) collective-permute-start(bf16[128,1024]{1,0:T(8,128)(2,1)S(1)} %slice.88), channel_id=1, source_target_pairs={{0,1},{1,0},{2,3},{3,2},{4,5},{5,4},{6,7},{7,6},{8,9},{9,8},{10,11... | collective-permute-start | bytes 786440 | tf_op jit(solution)/shard_map/ppermute | solution.py:360
  133.2 31.9 %collective-permute-start.22 = (bf16[256,1024]{1,0:T(8,128)(2,1)S(1)}, bf16[256,1024]{1,0:T(8,128)(2,1)S(1)}, u32[]{:S(2)}, u32[]{:S(2)}) collective-permute-start(bf16[256,1024]{1,0:T(8,128)(2,1)S(1)} %fusion.4), channel_id=1, source_target_pairs={{0,4},{4,0},{1,5},{5,1},{2,6},{6,2},{3,7},{7,3},{8,12},{12,8},{9,1... | collective-permute-start | bytes 1572872 | tf_op jit(solution)/shard_map/ppermute | solution.py:360
  140.0 5.2 %collective-permute-start.32 = (bf16[256,1024]{1,0:T(8,128)(2,1)S(1)}, bf16[256,1024]{1,0:T(8,128)(2,1)S(1)}, u32[]{:S(2)}, u32[]{:S(2)}) collective-permute-start(bf16[256,1024]{1,0:T(8,128)(2,1)S(1)} %constant_dynamic-update-slice_fusion.4), channel_id=1, source_target_pairs={{0,4},{4,0},{1,5},{5,1},{2,6},{6,2},{3,7},{7,3},{8,12},{12,8},{9,1... | collective-permute-start | bytes 1572872 | tf_op jit(solution)/shard_map/ppermute | solution.py:360
  140.5 1.4 copy-start
  143.1 5.3 %collective-permute-start.29 = (bf16[256,1024]{1,0:T(8,128)(2,1)S(1)}, bf16[256,1024]{1,0:T(8,128)(2,1)S(1)}, u32[]{:S(2)}, u32[]{:S(2)}) collective-permute-start(bf16[256,1024]{1,0:T(8,128)(2,1)S(1)} %fusion.6), channel_id=1, source_target_pairs={{0,4},{4,0},{1,5},{5,1},{2,6},{6,2},{3,7},{7,3},{8,12},{12,8},{9,1... | collective-permute-start | bytes 1572872 | tf_op jit(solution)/shard_map/ppermute | solution.py:360
  147.3 3.1 %collective-permute-start.34 = (bf16[256,1024]{1,0:T(8,128)(2,1)S(1)}, bf16[256,1024]{1,0:T(8,128)(2,1)S(1)}, u32[]{:S(2)}, u32[]{:S(2)}) collective-permute-start(bf16[256,1024]{1,0:T(8,128)(2,1)S(1)} %fusion.7), channel_id=1, source_target_pairs={{0,4},{4,0},{1,5},{5,1},{2,6},{6,2},{3,7},{7,3},{8,12},{12,8},{9,1... | collective-permute-start | bytes 1572872 | tf_op jit(solution)/shard_map/ppermute | solution.py:360
  147.8 4.9 %collective-permute-start.25 = (bf16[256,1024]{1,0:T(8,128)(2,1)S(1)}, bf16[256,1024]{1,0:T(8,128)(2,1)S(1)}, u32[]{:S(2)}, u32[]{:S(2)}) collective-permute-start(bf16[256,1024]{1,0:T(8,128)(2,1)S(1)} %fusion.5), channel_id=1, source_target_pairs={{0,4},{4,0},{1,5},{5,1},{2,6},{6,2},{3,7},{7,3},{8,12},{12,8},{9,1... | collective-permute-start | bytes 1572872 | tf_op jit(solution)/shard_map/ppermute | solution.py:360
  148.9 16.4 %collective-permute-start.38 = (bf16[128,1024]{1,0:T(8,128)(2,1)S(1)}, bf16[128,1024]{1,0:T(8,128)(2,1)S(1)}, u32[]{:S(2)}, u32[]{:S(2)}) collective-permute-start(bf16[128,1024]{1,0:T(8,128)(2,1)S(1)} %slice.162), channel_id=1, source_target_pairs={{0,2},{1,3},{2,0},{3,1},{4,6},{5,7},{6,4},{7,5},{8,10},{9,11},{10,... | collective-permute-start | bytes 786440 | tf_op jit(solution)/shard_map/ppermute | solution.py:360
  150.9 9.2 %collective-permute-start.35 = (bf16[128,1024]{1,0:T(8,128)(2,1)S(1)}, bf16[128,1024]{1,0:T(8,128)(2,1)S(1)}, u32[]{:S(2)}, u32[]{:S(2)}) collective-permute-start(bf16[128,1024]{1,0:T(8,128)(2,1)S(1)} %get-tuple-element.60), channel_id=1, source_target_pairs={{0,1},{1,0},{2,3},{3,2},{4,5},{5,4},{6,7},{7,6},{8,9},{9,8},{10,11... | collective-permute-start | bytes 786440 | tf_op jit(solution)/shard_map/ppermute | solution.py:360
  152.0 11.7 %collective-permute-start.39 = (bf16[128,1024]{1,0:T(8,128)(2,1)S(1)}, bf16[128,1024]{1,0:T(8,128)(2,1)S(1)}, u32[]{:S(2)}, u32[]{:S(2)}) collective-permute-start(bf16[128,1024]{1,0:T(8,128)(2,1)S(1)} %get-tuple-element.59), channel_id=1, source_target_pairs={{0,2},{1,3},{2,0},{3,1},{4,6},{5,7},{6,4},{7,5},{8,10},{9,11},{10,... | collective-permute-start | bytes 786440 | tf_op jit(solution)/shard_map/ppermute | solution.py:360
  153.2 12.0 %collective-permute-start.26 = (bf16[128,1024]{1,0:T(8,128)(2,1)S(1)}, bf16[128,1024]{1,0:T(8,128)(2,1)S(1)}, u32[]{:S(2)}, u32[]{:S(2)}) collective-permute-start(bf16[128,1024]{1,0:T(8,128)(2,1)S(1)} %slice.163), channel_id=1, source_target_pairs={{0,1},{1,0},{2,3},{3,2},{4,5},{5,4},{6,7},{7,6},{8,9},{9,8},{10,11... | collective-permute-start | bytes 786440 | tf_op jit(solution)/shard_map/ppermute | solution.py:360
  160.2 8.3 %collective-permute-start.36 = (bf16[128,1024]{1,0:T(8,128)(2,1)S(1)}, bf16[128,1024]{1,0:T(8,128)(2,1)S(1)}, u32[]{:S(2)}, u32[]{:S(2)}) collective-permute-start(bf16[128,1024]{1,0:T(8,128)(2,1)S(1)} %fusion.55), channel_id=1, source_target_pairs={{0,2},{1,3},{2,0},{3,1},{4,6},{5,7},{6,4},{7,5},{8,10},{9,11},{10,... | collective-permute-start | bytes 786440 | tf_op jit(solution)/shard_map/ppermute | solution.py:360
  163.8 6.5 %collective-permute-start.40 = (bf16[128,1024]{1,0:T(8,128)(2,1)S(1)}, bf16[128,1024]{1,0:T(8,128)(2,1)S(1)}, u32[]{:S(2)}, u32[]{:S(2)}) collective-permute-start(bf16[128,1024]{1,0:T(8,128)(2,1)S(1)} %fusion.52), channel_id=1, source_target_pairs={{0,1},{1,0},{2,3},{3,2},{4,5},{5,4},{6,7},{7,6},{8,9},{9,8},{10,11... | collective-permute-start | bytes 786440 | tf_op jit(solution)/shard_map/ppermute | solution.py:360
  170.6 10.6 %collective-permute-start.41 = (bf16[64,1024]{1,0:T(8,128)(2,1)S(1)}, bf16[64,1024]{1,0:T(8,128)(2,1)S(1)}, u32[]{:S(2)}, u32[]{:S(2)}) collective-permute-start(bf16[64,1024]{1,0:T(8,128)(2,1)S(1)} %get-tuple-element.64), channel_id=1, source_target_pairs={{0,16},{8,24},{16,0},{24,8},{1,17},{9,25},{17,1},{25,9},{2,18},{10... | collective-permute-start | bytes 393224 | tf_op jit(solution)/shard_map/ppermute | solution.py:347
  172.2 9.0 %collective-permute-start.42 = (bf16[64,1024]{1,0:T(8,128)(2,1)S(1)}, bf16[64,1024]{1,0:T(8,128)(2,1)S(1)}, u32[]{:S(2)}, u32[]{:S(2)}) collective-permute-start(bf16[64,1024]{1,0:T(8,128)(2,1)S(1)} %get-tuple-element.65), channel_id=1, source_target_pairs={{0,8},{8,16},{16,24},{24,0},{1,9},{9,17},{17,25},{25,1},{2,10},{10... | collective-permute-start | bytes 393224 | tf_op jit(solution)/shard_map/ppermute | solution.py:347
  174.4 7.1 %collective-permute-start.37 = (bf16[64,1024]{1,0:T(8,128)(2,1)S(1)}, bf16[64,1024]{1,0:T(8,128)(2,1)S(1)}, u32[]{:S(2)}, u32[]{:S(2)}) collective-permute-start(bf16[64,1024]{1,0:T(8,128)(2,1)S(1)} %slice.164), channel_id=1, source_target_pairs={{0,24},{8,0},{16,8},{24,16},{1,25},{9,1},{17,9},{25,17},{2,26},{10... | collective-permute-start | bytes 393224 | tf_op jit(solution)/shard_map/ppermute | solution.py:347

commit v2 on v0

--- a/solution.py
+++ b/solution.py
@@ -544,9 +544,8 @@
         shift(take_block(split_weight, targets[s]), "exp", s) for s in range(1, exp_size)
     ]
     if dense:
-        column_table = jnp.stack(gather_blocks(route_table(route_ids, route_weights), "req"))
-        own_piece, column_table, flat_in = lax.optimization_barrier(
-            (pieces[0][0], column_table, expert_in[0].reshape(model_width, -1))
+        own_piece, flat_in = lax.optimization_barrier(
+            (pieces[0][0], expert_in[0].reshape(model_width, -1))
         )
         pieces[0] = [own_piece] + pieces[0][1:]
     received = []
@@ -555,16 +554,19 @@
             gathered, sources, new_keys, new_values, key_cache, value_cache, local_lengths,
             start, 512, 256,
         )
-        received.append(
-            [messages[0]] + [shift(messages[s], "exp", s) for s in range(1, exp_size)]
-        )
+        sent = [messages[0]]
+        for s in range(1, exp_size):
+            sent.append(shift(messages[s], "exp", s))
+        received.append(sent)
     if dense:
         maps_in = halves(flat_in, half_width, 0)
         maps_out = halves(expert_out[0], half_width, 1)
         gains = halves(norm_gain, half_width, 0)
-        own_message, maps_in, maps_out = lax.optimization_barrier(
-            (received[-1][0], maps_in, maps_out)
-        )
+        own_message, named, given = lax.optimization_barrier(
+            (received[-1][0], route_ids, route_weights)
+        )
+        column_table = jnp.stack(gather_blocks(route_table(named, given), "req"))
+        own_message, maps_in, maps_out = lax.optimization_barrier((own_message, maps_in, maps_out))
         received[-1] = [own_message] + received[-1][1:]
     group_shift = (head_size - (exp_at * share) % group) % head_size
     info = jnp.concatenate([jnp.stack([group_shift, head_at]).astype(jnp.int32), sources])

time: 198 us -> 187 us (0.944)
  waiting for transfers between devices: 66.5 us -> 59.1 us
  starting transfers between devices: 52.4 us -> 49.6 us
    ppermute x22, waiting for transfers between devices: 31.2 us -> 21.8 us  [shift(): lax.ppermute(value, axis, [(i, (i + step) % size) for i in range(size)])]
    ppermute x21, starting transfers between devices: 15.4 us -> 12.4 us  [swap(): return lax.ppermute(value, axis, [(i, i ^ bits) for i in range(size)])]
    ppermute x21, waiting for transfers between devices: 35.3 us -> 37.3 us  [swap(): return lax.ppermute(value, axis, [(i, i ^ bits) for i in range(size)])]
  transfers between devices with their start and end apart: 43 -> 43, of which waited for: 19 -> 18; matrix products, arithmetic and copies ran while one was open for 14% -> 15% of each run, Pallas kernels for 20% -> 21%
where the time goes in v2:
time: 187 us; the launch traced here: 186 us
  waiting for transfers between devices  59.1 us (32%)
  starting transfers between devices  49.6 us (27%)
  Pallas kernels  44.5 us (24%)
  local copies, waits for them, and re-layouts  16.4 us (9%)
  matrix products  8.55 us (5%)
  other arithmetic  7.61 us (4%)
    pallas_call x1, Pallas kernels, attend(): pl.pallas_call(functools.partial(attend_kernel, pieces, base, listed, sub...  39.4 us
    ppermute x21, waiting for transfers between devices, swap(): return lax.ppermute(value, axis, [(i, i ^ bits) for i in range(size)])  37.3 us
    ppermute x22, starting transfers between devices, shift(): lax.ppermute(value, axis, [(i, (i + step) % size) for i in range(size)])  37.2 us
    ppermute x22, waiting for transfers between devices, shift(): lax.ppermute(value, axis, [(i, (i + step) % size) for i in range(size)])  21.8 us
    ppermute x21, starting transfers between devices, swap(): return lax.ppermute(value, axis, [(i, i ^ bits) for i in range(size)])  12.4 us
    unnamed x23, local copies, waits for them, and re-layouts  5.37 us
    pallas_call x1, Pallas kernels, merge_project(): pl.pallas_call(functools.partial(merge_kernel, parts, len(batches), share...  5.08 us
  transfers between devices with their start and end apart: 43, of which 18 were waited for; matrix products, arithmetic and copies ran while one was open for 15% of the time, Pallas kernels for 21%

profile of v2, /device:TPU:0, one launch (start us, length us, event | category | flops | bytes accessed | tf_op | source)
XLA Modules:
  0.0 186.2 jit_solution(15091222731205762724)
XLA Ops:
  0.0 3.0 %collective-permute-start = (bf16[4,16,16,128]{3,2,1,0:T(8,128)(2,1)}, bf16[4,16,16,128]{3,2,1,0:T(8,128)(2,1)S(1)}, u32[]{:S(2)}, u32[]{:S(2)}) collective-permute-start(bf16[4,16,16,128]{3,2,1,0:T(8,128)(2,1)} %refs_0_), channel_id=1, source_target_pairs={{0,1},{1,2},{2,3},{3,0},{4,5},{5,6},{6,7},{7,4},{8,9},{9,10},{10,1... | collective-permute-start | bytes 786440 | tf_op jit(solution)/shard_map/ppermute | solution.py:347
  3.0 1.5 collective-permute-start.1
  4.5 1.4 collective-permute-start.2
  5.9 2.9 %dynamic-slice_bitcast_fusion.2 = (bf16[512,512]{1,0:T(8,128)(2,1)}, bf16[512,512]{1,0:T(8,128)(2,1)}, bf16[512,512]{1,0:T(8,128)(2,1)}, bf16[512,512]{1,0:T(8,128)(2,1)}) fusion(bf16[4,512,512]{2,1,0:T(8,128)(2,1)} %bitcast.75, s32[]{:T(128)S(6)} %select_n.92, s32[]{:T(128)S(6)} %select_n.90, s32[]{:T(128)S(6)} %select_n.88, s32[]{:T(128)S(6)} %select_n.86), kind=kLoop, calls=%fused_computation.96 | loop fusion | bytes 4194320 | tf_op jit(solution)/shard_map/jit(dynamic_index_in_dim)/squeeze | solution.py:351
  10.0 4.3 %copy.16 = bf16[256,8,2,384]{3,1,2,0:T(8,128)(2,1)} copy(bf16[256,8,2,384]{3,2,1,0:T(2,128)(2,1)} %bitcast.74) | data formatting | bytes 6291456
  14.3 1.9 %collective-permute-start.8 = (bf16[512,512]{1,0:T(8,128)(2,1)}, bf16[512,512]{1,0:T(8,128)(2,1)}, u32[]{:S(2)}, u32[]{:S(2)}) collective-permute-start(bf16[512,512]{1,0:T(8,128)(2,1)} %get-tuple-element.61), channel_id=1, source_target_pairs={{0,3},{1,0},{2,1},{3,2},{4,7},{5,4},{6,5},{7,6},{8,11},{9,8},{10,9... | collective-permute-start | bytes 1572872 | tf_op jit(solution)/shard_map/ppermute | solution.py:347
  17.6 39.4 %attend.1 = (bf16[64,2176]{1,0:T(8,128)(2,1)}, bf16[64,2176]{1,0:T(8,128)(2,1)}, bf16[64,2176]{1,0:T(8,128)(2,1)}, bf16[64,2176]{1,0:T(8,128)(2,1)}) custom-call(s32[8]{0:T(128)} %pad_add_fusion.1.info_ref, bf16[4,16,16,128]{3,2,1,0:T(8,128)(2,1)} %refs_0_, bf16[4,16,16,128]{3,2,1,0:T(8,128)(2,1)} %copy-done.4, ...), custom_call_target="tpu_custom_call" | custom-call | tf_op jit(solution)/shard_map/attend/pallas_call | solution.py:243
  57.1 2.8 %collective-permute-start.5 = (bf16[64,2176]{1,0:T(8,128)(2,1)}, bf16[64,2176]{1,0:T(8,128)(2,1)}, u32[]{:S(2)}, u32[]{:S(2)}) collective-permute-start(bf16[64,2176]{1,0:T(8,128)(2,1)} %get-tuple-element.38), channel_id=1, source_target_pairs={{0,3},{1,0},{2,1},{3,2},{4,7},{5,4},{6,5},{7,6},{8,11},{9,8},{10,9... | collective-permute-start | bytes 835592 | tf_op jit(solution)/shard_map/ppermute | solution.py:347
  59.9 0.6 pad_add_fusion.info_ref
  60.5 3.2 %constant_dynamic-slice_fusion.4 = (bf16[1024,768]{1,0:T(8,128)(2,1)}, bf16[1024,768]{1,0:T(8,128)(2,1)S(1)}) fusion(bf16[2048,768]{1,0:T(8,128)(2,1)} %bitcast.71, s32[]{:T(128)S(6)} %select_n.84, s32[]{:T(128)S(6)} %select_n.80), kind=kLoop, calls=%fused_computation.134 | loop fusion | bytes 6291464 | tf_op jit(solution)/shard_map/dynamic_slice | solution.py:391
  63.8 3.9 %collective-permute-done.3.refs_1_ = bf16[64,2176]{1,0:T(8,128)(2,1)S(1)} collective-permute-done((bf16[64,2176]{1,0:T(8,128)(2,1)}, bf16[64,2176]{1,0:T(8,128)(2,1)S(1)}, u32[]{:S(2)}, u32[]{:S(2)}) %collective-permute-start.3) | collective-permute-done | bytes 278560 | tf_op jit(solution)/shard_map/ppermute | solution.py:347
  67.6 3.6 %collective-permute-done.4.refs_2_ = bf16[64,2176]{1,0:T(8,128)(2,1)} collective-permute-done((bf16[64,2176]{1,0:T(8,128)(2,1)}, bf16[64,2176]{1,0:T(8,128)(2,1)}, u32[]{:S(2)}, u32[]{:S(2)}) %collective-permute-start.4) | collective-permute-done | bytes 278560 | tf_op jit(solution)/shard_map/ppermute | solution.py:347
  71.2 5.1 %merge_project.1 = (f32[256,1024]{1,0:T(8,128)}, bf16[256,1024]{1,0:T(8,128)(2,1)}) custom-call(s32[6]{0:T(128)} %pad_add_fusion.info_ref, bf16[64,2176]{1,0:T(8,128)(2,1)} %get-tuple-element.35.refs_0_, bf16[64,2176]{1,0:T(8,128)(2,1)} %copy-done.3, bf16[64,2176]{1,0:T(8,128)(2,1)} %collective-permute-done.4.refs_2_, ...), custom_call_target="tpu_custom_call" | custom-call | tf_op jit(solution)/shard_map/merge_project/pallas_call | solution.py:327
  76.4 8.1 %collective-permute-start.9 = (f32[16,64]{1,0:T(8,128)S(1)}, f32[16,64]{1,0:T(8,128)S(1)}, u32[]{:S(2)}, u32[]{:S(2)}) collective-permute-start(f32[16,64]{1,0:T(8,128)S(1)} %select_reduce_fusion), channel_id=1, source_target_pairs={{0,8},{8,16},{16,24},{24,0},{1,9},{9,17},{17,25},{25,1},{2,10},{10... | collective-permute-start | bytes 12296 | tf_op jit(solution)/shard_map/ppermute | solution.py:347
  84.4 0.7 collective-permute-start.10
  85.2 1.7 collective-permute-start.11
  86.9 2.1 %collective-permute-done.10 = f32[16,64]{1,0:T(8,128)S(1)} collective-permute-done((f32[16,64]{1,0:T(8,128)S(1)}, f32[16,64]{1,0:T(8,128)S(1)}, u32[]{:S(2)}, u32[]{:S(2)}) %collective-permute-start.10) | collective-permute-done | bytes 4128 | tf_op jit(solution)/shard_map/ppermute | solution.py:347
  89.0 0.6 pad_maximum_fusion
  89.6 1.4 convert_add_fusion.3
  91.0 1.0 copy-done.1
  92.1 1.4 collective-permute-start.13
  93.5 1.8 collective-permute-start.14
  95.3 1.2 collective-permute-start.15
  96.5 1.5 constant_dynamic-slice_fusion
  98.0 0.8 collective-permute-start.16
  99.1 2.5 %collective-permute-done.16 = f32[4,64]{1,0:T(4,128)S(1)} collective-permute-done((f32[4,64]{1,0:T(4,128)S(1)}, f32[4,64]{1,0:T(4,128)S(1)}, u32[]{:S(2)}, u32[]{:S(2)}) %collective-permute-start.16) | collective-permute-done | bytes 1056 | tf_op jit(solution)/shard_map/ppermute | solution.py:360
  102.2 0.8 reshape.106
  103.0 0.8 reshape.107
  103.7 2.6 %collective-permute-done.18 = f32[4,64]{1,0:T(4,128)} collective-permute-done((f32[4,64]{1,0:T(4,128)}, f32[4,64]{1,0:T(4,128)}, u32[]{:S(2)}, u32[]{:S(2)}) %collective-permute-start.18) | collective-permute-done | bytes 1056 | tf_op jit(solution)/shard_map/ppermute | solution.py:360
  106.4 0.8 reshape.108
  107.1 1.4 fusion.82
  108.5 0.7 collective-permute-start.19
  109.2 3.3 %collective-permute-start.20 = (bf16[64,1024]{1,0:T(8,128)(2,1)S(1)}, bf16[64,1024]{1,0:T(8,128)(2,1)S(1)}, u32[]{:S(2)}, u32[]{:S(2)}) collective-permute-start(bf16[64,1024]{1,0:T(8,128)(2,1)S(1)} %get-tuple-element.45), channel_id=1, source_target_pairs={{0,16},{8,24},{16,0},{24,8},{1,17},{9,25},{17,1},{25,9},{2,18},{10... | collective-permute-start | bytes 393224 | tf_op jit(solution)/shard_map/ppermute | solution.py:347
  112.5 1.3 collective-permute-start.21
  113.7 1.7 collective-permute-done.19
  115.4 3.9 %collective-permute-done.20 = bf16[64,1024]{1,0:T(8,128)(2,1)S(1)} collective-permute-done((bf16[64,1024]{1,0:T(8,128)(2,1)S(1)}, bf16[64,1024]{1,0:T(8,128)(2,1)S(1)}, u32[]{:S(2)}, u32[]{:S(2)}) %collective-permute-start.20) | collective-permute-done | bytes 131104 | tf_op jit(solution)/shard_map/ppermute | solution.py:347
  119.5 0.7 fusion.86
  120.2 0.9 collective-permute-start.23
  121.9 0.6 fusion.41
  122.5 0.6 fusion.45
  123.8 10.8 %collective-permute-done.23 = bf16[256,1024]{1,0:T(8,128)(2,1)S(1)} collective-permute-done((bf16[256,1024]{1,0:T(8,128)(2,1)S(1)}, bf16[256,1024]{1,0:T(8,128)(2,1)S(1)}, u32[]{:S(2)}, u32[]{:S(2)}) %collective-permute-start.23) | collective-permute-done | bytes 524320 | tf_op jit(solution)/shard_map/ppermute | solution.py:360
  134.5 0.6 collective-permute-done.24
  136.3 1.1 collective-permute-start.32
  137.6 5.1 %collective-permute-done.31 = bf16[128,1024]{1,0:T(8,128)(2,1)S(1)} collective-permute-done((bf16[128,1024]{1,0:T(8,128)(2,1)S(1)}, bf16[128,1024]{1,0:T(8,128)(2,1)S(1)}, u32[]{:S(2)}, u32[]{:S(2)}) %collective-permute-start.31) | collective-permute-done | bytes 262176 | tf_op jit(solution)/shard_map/ppermute | solution.py:360
  142.8 1.7 collective-permute-done.32
  145.0 0.6 fusion.36
  145.7 0.6 convolution_add_fusion
  147.6 0.6 fusion.39
  148.3 0.6 convolution_add_fusion.1
  149.2 0.6 fusion.28
  149.9 0.6 fusion.32
  152.7 1.7 collective-permute-start.38
  154.8 1.2 collective-permute-start.35
  156.9 1.0 collective-permute-start.28
  157.9 6.2 %collective-permute-done.35 = bf16[128,1024]{1,0:T(8,128)(2,1)S(1)} collective-permute-done((bf16[128,1024]{1,0:T(8,128)(2,1)S(1)}, bf16[128,1024]{1,0:T(8,128)(2,1)S(1)}, u32[]{:S(2)}, u32[]{:S(2)}) %collective-permute-start.35) | collective-permute-done | bytes 262176 | tf_op jit(solution)/shard_map/ppermute | solution.py:360
  164.6 2.9 %collective-permute-done.39 = bf16[128,1024]{1,0:T(8,128)(2,1)S(1)} collective-permute-done((bf16[128,1024]{1,0:T(8,128)(2,1)S(1)}, bf16[128,1024]{1,0:T(8,128)(2,1)S(1)}, u32[]{:S(2)}, u32[]{:S(2)}) %collective-permute-start.39) | collective-permute-done | bytes 262176 | tf_op jit(solution)/shard_map/ppermute | solution.py:360
  167.6 1.2 collective-permute-start.40
  169.2 3.0 %collective-permute-done.36 = bf16[128,1024]{1,0:T(8,128)(2,1)S(1)} collective-permute-done((bf16[128,1024]{1,0:T(8,128)(2,1)S(1)}, bf16[128,1024]{1,0:T(8,128)(2,1)S(1)}, u32[]{:S(2)}, u32[]{:S(2)}) %collective-permute-start.36) | collective-permute-done | bytes 262176 | tf_op jit(solution)/shard_map/ppermute | solution.py:360
  172.2 1.9 %collective-permute-done.40 = bf16[128,1024]{1,0:T(8,128)(2,1)S(1)} collective-permute-done((bf16[128,1024]{1,0:T(8,128)(2,1)S(1)}, bf16[128,1024]{1,0:T(8,128)(2,1)S(1)}, u32[]{:S(2)}, u32[]{:S(2)}) %collective-permute-start.40) | collective-permute-done | bytes 262176 | tf_op jit(solution)/shard_map/ppermute | solution.py:360
  174.3 1.3 collective-permute-start.41
  175.7 2.3 %collective-permute-start.42 = (bf16[64,1024]{1,0:T(8,128)(2,1)S(1)}, bf16[64,1024]{1,0:T(8,128)(2,1)S(1)}, u32[]{:S(2)}, u32[]{:S(2)}) collective-permute-start(bf16[64,1024]{1,0:T(8,128)(2,1)S(1)} %get-tuple-element.75), channel_id=1, source_target_pairs={{0,8},{8,16},{16,24},{24,0},{1,9},{9,17},{17,25},{25,1},{2,10},{10... | collective-permute-start | bytes 393224 | tf_op jit(solution)/shard_map/ppermute | solution.py:347
  177.9 1.6 collective-permute-start.37
  179.6 5.9 %collective-permute-done.41 = bf16[64,1024]{1,0:T(8,128)(2,1)S(1)} collective-permute-done((bf16[64,1024]{1,0:T(8,128)(2,1)S(1)}, bf16[64,1024]{1,0:T(8,128)(2,1)S(1)}, u32[]{:S(2)}, u32[]{:S(2)}) %collective-permute-start.41) | collective-permute-done | bytes 131104 | tf_op jit(solution)/shard_map/ppermute | solution.py:347
  185.5 0.7 fusion.76
  (110 shorter events, 13.5 us)
Async XLA Ops:
  0.0 14.3 %collective-permute-start = (bf16[4,16,16,128]{3,2,1,0:T(8,128)(2,1)}, bf16[4,16,16,128]{3,2,1,0:T(8,128)(2,1)S(1)}, u32[]{:S(2)}, u32[]{:S(2)}) collective-permute-start(bf16[4,16,16,128]{3,2,1,0:T(8,128)(2,1)} %refs_0_), channel_id=1, source_target_pairs={{0,1},{1,2},{2,3},{3,0},{4,5},{5,6},{6,7},{7,4},{8,9},{9,10},{10,1... | collective-permute-start | bytes 786440 | tf_op jit(solution)/shard_map/ppermute | solution.py:347
  3.0 14.1 %collective-permute-start.1 = (bf16[4,16,16,128]{3,2,1,0:T(8,128)(2,1)}, bf16[4,16,16,128]{3,2,1,0:T(8,128)(2,1)}, u32[]{:S(2)}, u32[]{:S(2)}) collective-permute-start(bf16[4,16,16,128]{3,2,1,0:T(8,128)(2,1)} %refs_0_), channel_id=1, source_target_pairs={{0,2},{1,3},{2,0},{3,1},{4,6},{5,7},{6,4},{7,5},{8,10},{9,11},{10,... | collective-permute-start | bytes 786440 | tf_op jit(solution)/shard_map/ppermute | solution.py:347
  4.5 13.1 %collective-permute-start.2 = (bf16[4,16,16,128]{3,2,1,0:T(8,128)(2,1)}, bf16[4,16,16,128]{3,2,1,0:T(8,128)(2,1)}, u32[]{:S(2)}, u32[]{:S(2)}) collective-permute-start(bf16[4,16,16,128]{3,2,1,0:T(8,128)(2,1)} %refs_0_), channel_id=1, source_target_pairs={{0,3},{1,0},{2,1},{3,2},{4,7},{5,4},{6,5},{7,6},{8,11},{9,8},{10,9... | collective-permute-start | bytes 786440 | tf_op jit(solution)/shard_map/ppermute | solution.py:347
  8.8 48.3 %collective-permute-start.6 = (bf16[512,512]{1,0:T(8,128)(2,1)}, bf16[512,512]{1,0:T(8,128)(2,1)}, u32[]{:S(2)}, u32[]{:S(2)}) collective-permute-start(bf16[512,512]{1,0:T(8,128)(2,1)} %get-tuple-element.63), channel_id=1, source_target_pairs={{0,1},{1,2},{2,3},{3,0},{4,5},{5,6},{6,7},{7,4},{8,9},{9,10},{10,1... | collective-permute-start | bytes 1572872 | tf_op jit(solution)/shard_map/ppermute | solution.py:347
  9.4 54.4 %collective-permute-start.7 = (bf16[512,512]{1,0:T(8,128)(2,1)}, bf16[512,512]{1,0:T(8,128)(2,1)}, u32[]{:S(2)}, u32[]{:S(2)}) collective-permute-start(bf16[512,512]{1,0:T(8,128)(2,1)} %get-tuple-element.62), channel_id=1, source_target_pairs={{0,2},{1,3},{2,0},{3,1},{4,6},{5,7},{6,4},{7,5},{8,10},{9,11},{10,... | collective-permute-start | bytes 1572872 | tf_op jit(solution)/shard_map/ppermute | solution.py:347
  9.9 4.3 %copy-start.8 = (s32[4]{0:T(128)S(1)}, s32[4]{0:T(128)}, u32[]{:S(2)}) copy-start(s32[4]{0:T(128)} %param.18) | copy-start | bytes 52
  10.0 6.8 %copy-start.2 = (bf16[1,384,2048]{2,1,0:T(8,128)(2,1)S(1)}, bf16[1,384,2048]{2,1,0:T(8,128)(2,1)}, u32[]{:S(2)}) copy-start(bf16[1,384,2048]{2,1,0:T(8,128)(2,1)} %param.25) | copy-start | bytes 4718596
  14.3 2.7 %copy-start.4 = (bf16[4,16,16,128]{3,2,1,0:T(8,128)(2,1)}, bf16[4,16,16,128]{3,2,1,0:T(8,128)(2,1)S(1)}, u32[]{:S(2)}) copy-start(bf16[4,16,16,128]{3,2,1,0:T(8,128)(2,1)S(1)} %collective-permute-done.refs_1_) | copy-start | bytes 786436
  14.3 49.5 %collective-permute-start.8 = (bf16[512,512]{1,0:T(8,128)(2,1)}, bf16[512,512]{1,0:T(8,128)(2,1)}, u32[]{:S(2)}, u32[]{:S(2)}) collective-permute-start(bf16[512,512]{1,0:T(8,128)(2,1)} %get-tuple-element.61), channel_id=1, source_target_pairs={{0,3},{1,0},{2,1},{3,2},{4,7},{5,4},{6,5},{7,6},{8,11},{9,8},{10,9... | collective-permute-start | bytes 1572872 | tf_op jit(solution)/shard_map/ppermute | solution.py:347
  57.0 10.6 %collective-permute-start.3 = (bf16[64,2176]{1,0:T(8,128)(2,1)}, bf16[64,2176]{1,0:T(8,128)(2,1)S(1)}, u32[]{:S(2)}, u32[]{:S(2)}) collective-permute-start(bf16[64,2176]{1,0:T(8,128)(2,1)} %get-tuple-element.36), channel_id=1, source_target_pairs={{0,1},{1,2},{2,3},{3,0},{4,5},{5,6},{6,7},{7,4},{8,9},{9,10},{10,1... | collective-permute-start | bytes 835592 | tf_op jit(solution)/shard_map/ppermute | solution.py:347
  57.0 14.2 %collective-permute-start.4 = (bf16[64,2176]{1,0:T(8,128)(2,1)}, bf16[64,2176]{1,0:T(8,128)(2,1)}, u32[]{:S(2)}, u32[]{:S(2)}) collective-permute-start(bf16[64,2176]{1,0:T(8,128)(2,1)} %get-tuple-element.37), channel_id=1, source_target_pairs={{0,2},{1,3},{2,0},{3,1},{4,6},{5,7},{6,4},{7,5},{8,10},{9,11},{10,... | collective-permute-start | bytes 835592 | tf_op jit(solution)/shard_map/ppermute | solution.py:347
  57.1 14.1 %collective-permute-start.5 = (bf16[64,2176]{1,0:T(8,128)(2,1)}, bf16[64,2176]{1,0:T(8,128)(2,1)}, u32[]{:S(2)}, u32[]{:S(2)}) collective-permute-start(bf16[64,2176]{1,0:T(8,128)(2,1)} %get-tuple-element.38), channel_id=1, source_target_pairs={{0,3},{1,0},{2,1},{3,2},{4,7},{5,4},{6,5},{7,6},{8,11},{9,8},{10,9... | collective-permute-start | bytes 835592 | tf_op jit(solution)/shard_map/ppermute | solution.py:347
  67.6 3.6 %copy-start.3 = (bf16[64,2176]{1,0:T(8,128)(2,1)}, bf16[64,2176]{1,0:T(8,128)(2,1)S(1)}, u32[]{:S(2)}) copy-start(bf16[64,2176]{1,0:T(8,128)(2,1)S(1)} %collective-permute-done.3.refs_1_) | copy-start | bytes 835588
  71.2 5.1 %copy-start.5 = (f32[64,8]{0,1:T(8,128)S(1)}, f32[64,8]{0,1:T(8,128)}, u32[]{:S(2)}) copy-start(f32[64,8]{0,1:T(8,128)} %param.23) | copy-start | bytes 6148
  71.2 5.1 %copy-start.6 = (s32[64,8]{0,1:T(8,128)S(1)}, s32[64,8]{0,1:T(8,128)}, u32[]{:S(2)}) copy-start(s32[64,8]{0,1:T(8,128)} %param.22) | copy-start | bytes 6148
  76.3 13.3 %collective-permute-start.12 = (bf16[256,1024]{1,0:T(8,128)(2,1)}, bf16[256,1024]{1,0:T(8,128)(2,1)S(1)}, u32[]{:S(2)}, u32[]{:S(2)}) collective-permute-start(bf16[256,1024]{1,0:T(8,128)(2,1)} %get-tuple-element.43), channel_id=1, source_target_pairs={{0,4},{4,0},{1,5},{5,1},{2,6},{6,2},{3,7},{7,3},{8,12},{12,8},{9,1... | collective-permute-start | bytes 1572872 | tf_op jit(solution)/shard_map/ppermute | solution.py:347
  76.4 10.5 %collective-permute-start.9 = (f32[16,64]{1,0:T(8,128)S(1)}, f32[16,64]{1,0:T(8,128)S(1)}, u32[]{:S(2)}, u32[]{:S(2)}) collective-permute-start(f32[16,64]{1,0:T(8,128)S(1)} %select_reduce_fusion), channel_id=1, source_target_pairs={{0,8},{8,16},{16,24},{24,0},{1,9},{9,17},{17,25},{25,1},{2,10},{10... | collective-permute-start | bytes 12296 | tf_op jit(solution)/shard_map/ppermute | solution.py:347
  84.4 4.5 %collective-permute-start.10 = (f32[16,64]{1,0:T(8,128)S(1)}, f32[16,64]{1,0:T(8,128)S(1)}, u32[]{:S(2)}, u32[]{:S(2)}) collective-permute-start(f32[16,64]{1,0:T(8,128)S(1)} %select_reduce_fusion), channel_id=1, source_target_pairs={{0,16},{8,24},{16,0},{24,8},{1,17},{9,25},{17,1},{25,9},{2,18},{10... | collective-permute-start | bytes 12296 | tf_op jit(solution)/shard_map/ppermute | solution.py:347
  85.2 3.8 %collective-permute-start.11 = (f32[16,64]{1,0:T(8,128)S(1)}, f32[16,64]{1,0:T(8,128)S(1)}, u32[]{:S(2)}, u32[]{:S(2)}) collective-permute-start(f32[16,64]{1,0:T(8,128)S(1)} %select_reduce_fusion), channel_id=1, source_target_pairs={{0,24},{8,0},{16,8},{24,16},{1,25},{9,1},{17,9},{25,17},{2,26},{10... | collective-permute-start | bytes 12296 | tf_op jit(solution)/shard_map/ppermute | solution.py:347
  91.0 1.0 copy-start.1
  92.1 15.0 %collective-permute-start.13 = (bf16[64,1024]{1,0:T(8,128)(2,1)S(1)}, bf16[64,1024]{1,0:T(8,128)(2,1)}, u32[]{:S(2)}, u32[]{:S(2)}) collective-permute-start(bf16[64,1024]{1,0:T(8,128)(2,1)S(1)} %get-tuple-element.71), channel_id=1, source_target_pairs={{0,1},{1,2},{2,3},{3,0},{4,5},{5,6},{6,7},{7,4},{8,9},{9,10},{10,1... | collective-permute-start | bytes 393224 | tf_op jit(solution)/shard_map/ppermute | solution.py:347
  93.5 13.6 %collective-permute-start.14 = (bf16[64,1024]{1,0:T(8,128)(2,1)S(1)}, bf16[64,1024]{1,0:T(8,128)(2,1)}, u32[]{:S(2)}, u32[]{:S(2)}) collective-permute-start(bf16[64,1024]{1,0:T(8,128)(2,1)S(1)} %get-tuple-element.73), channel_id=1, source_target_pairs={{0,2},{1,3},{2,0},{3,1},{4,6},{5,7},{6,4},{7,5},{8,10},{9,11},{10,... | collective-permute-start | bytes 393224 | tf_op jit(solution)/shard_map/ppermute | solution.py:347
  95.3 11.8 %collective-permute-start.15 = (bf16[64,1024]{1,0:T(8,128)(2,1)S(1)}, bf16[64,1024]{1,0:T(8,128)(2,1)}, u32[]{:S(2)}, u32[]{:S(2)}) collective-permute-start(bf16[64,1024]{1,0:T(8,128)(2,1)S(1)} %get-tuple-element.72), channel_id=1, source_target_pairs={{0,3},{1,0},{2,1},{3,2},{4,7},{5,4},{6,5},{7,6},{8,11},{9,8},{10,9... | collective-permute-start | bytes 393224 | tf_op jit(solution)/shard_map/ppermute | solution.py:347
  98.0 3.6 %collective-permute-start.16 = (f32[4,64]{1,0:T(4,128)S(1)}, f32[4,64]{1,0:T(4,128)S(1)}, u32[]{:S(2)}, u32[]{:S(2)}) collective-permute-start(f32[4,64]{1,0:T(4,128)S(1)} %bitcast.83), channel_id=1, source_target_pairs={{0,1},{1,0},{2,3},{3,2},{4,5},{5,4},{6,7},{7,6},{8,9},{9,8},{10,11... | collective-permute-start | bytes 3080 | tf_op jit(solution)/shard_map/ppermute | solution.py:360
  98.8 4.2 %collective-permute-start.17 = (f32[4,64]{1,0:T(4,128)S(1)}, f32[4,64]{1,0:T(4,128)}, u32[]{:S(2)}, u32[]{:S(2)}) collective-permute-start(f32[4,64]{1,0:T(4,128)S(1)} %bitcast.82), channel_id=1, source_target_pairs={{0,2},{1,3},{2,0},{3,1},{4,6},{5,7},{6,4},{7,5},{8,10},{9,11},{10,... | collective-permute-start | bytes 3080 | tf_op jit(solution)/shard_map/ppermute | solution.py:360
  101.6 0.6 copy-start.7
  101.6 4.8 %collective-permute-start.18 = (f32[4,64]{1,0:T(4,128)}, f32[4,64]{1,0:T(4,128)}, u32[]{:S(2)}, u32[]{:S(2)}) collective-permute-start(f32[4,64]{1,0:T(4,128)} %bitcast.24), channel_id=1, source_target_pairs={{0,3},{1,2},{2,1},{3,0},{4,7},{5,6},{6,5},{7,4},{8,11},{9,10},{10,... | collective-permute-start | bytes 3080 | tf_op jit(solution)/shard_map/ppermute | solution.py:360
  107.1 14.8 %copy-start = (bf16[1024,768]{1,0:T(8,128)(2,1)S(1)}, bf16[1024,768]{1,0:T(8,128)(2,1)}, u32[]{:S(2)}) copy-start(bf16[1024,768]{1,0:T(8,128)(2,1)} %get-tuple-element.47) | copy-start | bytes 4718596
  108.5 6.9 %collective-permute-start.19 = (bf16[64,1024]{1,0:T(8,128)(2,1)S(1)}, bf16[64,1024]{1,0:T(8,128)(2,1)S(1)}, u32[]{:S(2)}, u32[]{:S(2)}) collective-permute-start(bf16[64,1024]{1,0:T(8,128)(2,1)S(1)} %get-tuple-element.45), channel_id=1, source_target_pairs={{0,8},{8,16},{16,24},{24,0},{1,9},{9,17},{17,25},{25,1},{2,10},{10... | collective-permute-start | bytes 393224 | tf_op jit(solution)/shard_map/ppermute | solution.py:347
  109.2 10.2 %collective-permute-start.20 = (bf16[64,1024]{1,0:T(8,128)(2,1)S(1)}, bf16[64,1024]{1,0:T(8,128)(2,1)S(1)}, u32[]{:S(2)}, u32[]{:S(2)}) collective-permute-start(bf16[64,1024]{1,0:T(8,128)(2,1)S(1)} %get-tuple-element.45), channel_id=1, source_target_pairs={{0,16},{8,24},{16,0},{24,8},{1,17},{9,25},{17,1},{25,9},{2,18},{10... | collective-permute-start | bytes 393224 | tf_op jit(solution)/shard_map/ppermute | solution.py:347
  112.5 6.9 %collective-permute-start.21 = (bf16[64,1024]{1,0:T(8,128)(2,1)S(1)}, bf16[64,1024]{1,0:T(8,128)(2,1)S(1)}, u32[]{:S(2)}, u32[]{:S(2)}) collective-permute-start(bf16[64,1024]{1,0:T(8,128)(2,1)S(1)} %get-tuple-element.45), channel_id=1, source_target_pairs={{0,24},{8,0},{16,8},{24,16},{1,25},{9,1},{17,9},{25,17},{2,26},{10... | collective-permute-start | bytes 393224 | tf_op jit(solution)/shard_map/ppermute | solution.py:347
  119.4 2.3 %collective-permute-start.22 = (bf16[256,1024]{1,0:T(8,128)(2,1)S(1)}, bf16[256,1024]{1,0:T(8,128)(2,1)S(1)}, u32[]{:S(2)}, u32[]{:S(2)}) collective-permute-start(bf16[256,1024]{1,0:T(8,128)(2,1)S(1)} %constant_dynamic-update-slice_fusion), channel_id=1, source_target_pairs={{0,4},{4,0},{1,5},{5,1},{2,6},{6,2},{3,7},{7,3},{8,12},{12,8},{9,1... | collective-permute-start | bytes 1572872 | tf_op jit(solution)/shard_map/ppermute | solution.py:360
  120.2 14.3 %collective-permute-start.23 = (bf16[256,1024]{1,0:T(8,128)(2,1)S(1)}, bf16[256,1024]{1,0:T(8,128)(2,1)S(1)}, u32[]{:S(2)}, u32[]{:S(2)}) collective-permute-start(bf16[256,1024]{1,0:T(8,128)(2,1)S(1)} %constant_dynamic-update-slice_fusion), channel_id=1, source_target_pairs={{0,1},{1,0},{2,3},{3,2},{4,5},{5,4},{6,7},{7,6},{8,9},{9,8},{10,11... | collective-permute-start | bytes 1572872 | tf_op jit(solution)/shard_map/ppermute | solution.py:360
  121.1 14.0 %collective-permute-start.24 = (bf16[256,1024]{1,0:T(8,128)(2,1)S(1)}, bf16[256,1024]{1,0:T(8,128)(2,1)S(1)}, u32[]{:S(2)}, u32[]{:S(2)}) collective-permute-start(bf16[256,1024]{1,0:T(8,128)(2,1)S(1)} %constant_dynamic-update-slice_fusion), channel_id=1, source_target_pairs={{0,2},{1,3},{2,0},{3,1},{4,6},{5,7},{6,4},{7,5},{8,10},{9,11},{10,... | collective-permute-start | bytes 1572872 | tf_op jit(solution)/shard_map/ppermute | solution.py:360
  135.2 7.6 %collective-permute-start.31 = (bf16[128,1024]{1,0:T(8,128)(2,1)S(1)}, bf16[128,1024]{1,0:T(8,128)(2,1)S(1)}, u32[]{:S(2)}, u32[]{:S(2)}) collective-permute-start(bf16[128,1024]{1,0:T(8,128)(2,1)S(1)} %slice.87), channel_id=1, source_target_pairs={{0,2},{1,3},{2,0},{3,1},{4,6},{5,7},{6,4},{7,5},{8,10},{9,11},{10,... | collective-permute-start | bytes 786440 | tf_op jit(solution)/shard_map/ppermute | solution.py:360
  135.7 9.2 %collective-permute-start.29 = (bf16[256,1024]{1,0:T(8,128)(2,1)S(1)}, bf16[256,1024]{1,0:T(8,128)(2,1)S(1)}, u32[]{:S(2)}, u32[]{:S(2)}) collective-permute-start(bf16[256,1024]{1,0:T(8,128)(2,1)S(1)} %collective-permute-done.24), channel_id=1, source_target_pairs={{0,4},{4,0},{1,5},{5,1},{2,6},{6,2},{3,7},{7,3},{8,12},{12,8},{9,1... | collective-permute-start | bytes 1572872 | tf_op jit(solution)/shard_map/ppermute | solution.py:360
  135.7 11.8 %collective-permute-start.26 = (bf16[256,1024]{1,0:T(8,128)(2,1)S(1)}, bf16[256,1024]{1,0:T(8,128)(2,1)S(1)}, u32[]{:S(2)}, u32[]{:S(2)}) collective-permute-start(bf16[256,1024]{1,0:T(8,128)(2,1)S(1)} %collective-permute-done.23), channel_id=1, source_target_pairs={{0,4},{4,0},{1,5},{5,1},{2,6},{6,2},{3,7},{7,3},{8,12},{12,8},{9,1... | collective-permute-start | bytes 1572872 | tf_op jit(solution)/shard_map/ppermute | solution.py:360
  136.3 8.3 %collective-permute-start.32 = (bf16[128,1024]{1,0:T(8,128)(2,1)S(1)}, bf16[128,1024]{1,0:T(8,128)(2,1)S(1)}, u32[]{:S(2)}, u32[]{:S(2)}) collective-permute-start(bf16[128,1024]{1,0:T(8,128)(2,1)S(1)} %slice.88), channel_id=1, source_target_pairs={{0,1},{1,0},{2,3},{3,2},{4,5},{5,4},{6,7},{7,6},{8,9},{9,8},{10,11... | collective-permute-start | bytes 786440 | tf_op jit(solution)/shard_map/ppermute | solution.py:360
  137.4 31.4 %collective-permute-start.25 = (bf16[256,1024]{1,0:T(8,128)(2,1)S(1)}, bf16[256,1024]{1,0:T(8,128)(2,1)S(1)}, u32[]{:S(2)}, u32[]{:S(2)}) collective-permute-start(bf16[256,1024]{1,0:T(8,128)(2,1)S(1)} %fusion), channel_id=1, source_target_pairs={{0,4},{4,0},{1,5},{5,1},{2,6},{6,2},{3,7},{7,3},{8,12},{12,8},{9,1... | collective-permute-start | bytes 1572872 | tf_op jit(solution)/shard_map/ppermute | solution.py:360
  144.6 4.5 %collective-permute-start.33 = (bf16[256,1024]{1,0:T(8,128)(2,1)S(1)}, bf16[256,1024]{1,0:T(8,128)(2,1)S(1)}, u32[]{:S(2)}, u32[]{:S(2)}) collective-permute-start(bf16[256,1024]{1,0:T(8,128)(2,1)S(1)} %constant_dynamic-update-slice_fusion.4), channel_id=1, source_target_pairs={{0,4},{4,0},{1,5},{5,1},{2,6},{6,2},{3,7},{7,3},{8,12},{12,8},{9,1... | collective-permute-start | bytes 1572872 | tf_op jit(solution)/shard_map/ppermute | solution.py:360
  146.9 5.3 %collective-permute-start.30 = (bf16[256,1024]{1,0:T(8,128)(2,1)S(1)}, bf16[256,1024]{1,0:T(8,128)(2,1)S(1)}, u32[]{:S(2)}, u32[]{:S(2)}) collective-permute-start(bf16[256,1024]{1,0:T(8,128)(2,1)S(1)} %fusion.2), channel_id=1, source_target_pairs={{0,4},{4,0},{1,5},{5,1},{2,6},{6,2},{3,7},{7,3},{8,12},{12,8},{9,1... | collective-permute-start | bytes 1572872 | tf_op jit(solution)/shard_map/ppermute | solution.py:360
  151.1 3.2 %collective-permute-start.34 = (bf16[256,1024]{1,0:T(8,128)(2,1)S(1)}, bf16[256,1024]{1,0:T(8,128)(2,1)S(1)}, u32[]{:S(2)}, u32[]{:S(2)}) collective-permute-start(bf16[256,1024]{1,0:T(8,128)(2,1)S(1)} %fusion.3), channel_id=1, source_target_pairs={{0,4},{4,0},{1,5},{5,1},{2,6},{6,2},{3,7},{7,3},{8,12},{12,8},{9,1... | collective-permute-start | bytes 1572872 | tf_op jit(solution)/shard_map/ppermute | solution.py:360
  151.6 4.8 %collective-permute-start.27 = (bf16[256,1024]{1,0:T(8,128)(2,1)S(1)}, bf16[256,1024]{1,0:T(8,128)(2,1)S(1)}, u32[]{:S(2)}, u32[]{:S(2)}) collective-permute-start(bf16[256,1024]{1,0:T(8,128)(2,1)S(1)} %fusion.1), channel_id=1, source_target_pairs={{0,4},{4,0},{1,5},{5,1},{2,6},{6,2},{3,7},{7,3},{8,12},{12,8},{9,1... | collective-permute-start | bytes 1572872 | tf_op jit(solution)/shard_map/ppermute | solution.py:360
  152.7 16.6 %collective-permute-start.38 = (bf16[128,1024]{1,0:T(8,128)(2,1)S(1)}, bf16[128,1024]{1,0:T(8,128)(2,1)S(1)}, u32[]{:S(2)}, u32[]{:S(2)}) collective-permute-start(bf16[128,1024]{1,0:T(8,128)(2,1)S(1)} %slice.162), channel_id=1, source_target_pairs={{0,2},{1,3},{2,0},{3,1},{4,6},{5,7},{6,4},{7,5},{8,10},{9,11},{10,... | collective-permute-start | bytes 786440 | tf_op jit(solution)/shard_map/ppermute | solution.py:360
  154.8 9.2 %collective-permute-start.35 = (bf16[128,1024]{1,0:T(8,128)(2,1)S(1)}, bf16[128,1024]{1,0:T(8,128)(2,1)S(1)}, u32[]{:S(2)}, u32[]{:S(2)}) collective-permute-start(bf16[128,1024]{1,0:T(8,128)(2,1)S(1)} %get-tuple-element.70), channel_id=1, source_target_pairs={{0,1},{1,0},{2,3},{3,2},{4,5},{5,4},{6,7},{7,6},{8,9},{9,8},{10,11... | collective-permute-start | bytes 786440 | tf_op jit(solution)/shard_map/ppermute | solution.py:360
  156.0 11.5 %collective-permute-start.39 = (bf16[128,1024]{1,0:T(8,128)(2,1)S(1)}, bf16[128,1024]{1,0:T(8,128)(2,1)S(1)}, u32[]{:S(2)}, u32[]{:S(2)}) collective-permute-start(bf16[128,1024]{1,0:T(8,128)(2,1)S(1)} %get-tuple-element.69), channel_id=1, source_target_pairs={{0,2},{1,3},{2,0},{3,1},{4,6},{5,7},{6,4},{7,5},{8,10},{9,11},{10,... | collective-permute-start | bytes 786440 | tf_op jit(solution)/shard_map/ppermute | solution.py:360
  156.9 12.3 %collective-permute-start.28 = (bf16[128,1024]{1,0:T(8,128)(2,1)S(1)}, bf16[128,1024]{1,0:T(8,128)(2,1)S(1)}, u32[]{:S(2)}, u32[]{:S(2)}) collective-permute-start(bf16[128,1024]{1,0:T(8,128)(2,1)S(1)} %slice.163), channel_id=1, source_target_pairs={{0,1},{1,0},{2,3},{3,2},{4,5},{5,4},{6,7},{7,6},{8,9},{9,8},{10,11... | collective-permute-start | bytes 786440 | tf_op jit(solution)/shard_map/ppermute | solution.py:360
  164.1 8.1 %collective-permute-start.36 = (bf16[128,1024]{1,0:T(8,128)(2,1)S(1)}, bf16[128,1024]{1,0:T(8,128)(2,1)S(1)}, u32[]{:S(2)}, u32[]{:S(2)}) collective-permute-start(bf16[128,1024]{1,0:T(8,128)(2,1)S(1)} %fusion.51), channel_id=1, source_target_pairs={{0,2},{1,3},{2,0},{3,1},{4,6},{5,7},{6,4},{7,5},{8,10},{9,11},{10,... | collective-permute-start | bytes 786440 | tf_op jit(solution)/shard_map/ppermute | solution.py:360
  167.6 6.5 %collective-permute-start.40 = (bf16[128,1024]{1,0:T(8,128)(2,1)S(1)}, bf16[128,1024]{1,0:T(8,128)(2,1)S(1)}, u32[]{:S(2)}, u32[]{:S(2)}) collective-permute-start(bf16[128,1024]{1,0:T(8,128)(2,1)S(1)} %fusion.48), channel_id=1, source_target_pairs={{0,1},{1,0},{2,3},{3,2},{4,5},{5,4},{6,7},{7,6},{8,9},{9,8},{10,11... | collective-permute-start | bytes 786440 | tf_op jit(solution)/shard_map/ppermute | solution.py:360
  174.3 11.2 %collective-permute-start.41 = (bf16[64,1024]{1,0:T(8,128)(2,1)S(1)}, bf16[64,1024]{1,0:T(8,128)(2,1)S(1)}, u32[]{:S(2)}, u32[]{:S(2)}) collective-permute-start(bf16[64,1024]{1,0:T(8,128)(2,1)S(1)} %get-tuple-element.74), channel_id=1, source_target_pairs={{0,16},{8,24},{16,0},{24,8},{1,17},{9,25},{17,1},{25,9},{2,18},{10... | collective-permute-start | bytes 393224 | tf_op jit(solution)/shard_map/ppermute | solution.py:347
  175.7 9.8 %collective-permute-start.42 = (bf16[64,1024]{1,0:T(8,128)(2,1)S(1)}, bf16[64,1024]{1,0:T(8,128)(2,1)S(1)}, u32[]{:S(2)}, u32[]{:S(2)}) collective-permute-start(bf16[64,1024]{1,0:T(8,128)(2,1)S(1)} %get-tuple-element.75), channel_id=1, source_target_pairs={{0,8},{8,16},{16,24},{24,0},{1,9},{9,17},{17,25},{25,1},{2,10},{10... | collective-permute-start | bytes 393224 | tf_op jit(solution)/shard_map/ppermute | solution.py:347
  177.9 7.6 %collective-permute-start.37 = (bf16[64,1024]{1,0:T(8,128)(2,1)S(1)}, bf16[64,1024]{1,0:T(8,128)(2,1)S(1)}, u32[]{:S(2)}, u32[]{:S(2)}) collective-permute-start(bf16[64,1024]{1,0:T(8,128)(2,1)S(1)} %slice.164), channel_id=1, source_target_pairs={{0,24},{8,0},{16,8},{24,16},{1,25},{9,1},{17,9},{25,17},{2,26},{10... | collective-permute-start | bytes 393224 | tf_op jit(solution)/shard_map/ppermute | solution.py:347
